TPU v7x, 32 devices: a whole 2x2x4 slice. The times are simulated.
32 devices in a mesh: date: 16 (over z, y, core), strip: 2 (over x).
Axes of the slice: x: 2, y: 2, z: 4, core: 2. Of those that a mesh axis runs over, the one named last changes fastest.
Arguments:
- acquisitions: bfloat16 [32, 2, 2, 344, 640], P('date', None, None, None, 'strip'), may hold values from -6 to 6
- shifts: int32 [2, 32, 2, 5, 10], P(None, 'date', None, None, 'strip'), may hold values from -8 to 8, as said below
- fractions: int32 [2, 32, 2, 5, 10], P(None, 'date', None, None, 'strip'), may hold values from 0 to 63
- ref_dates: int32 [2], replicated, may hold values from 0 to 31, as said below
Outputs:
- chip_corr: float32 [2, 32, 2, 5, 10], P(None, 'date', None, None, 'strip')
- coherence: float32 [2, 31, 2, 64, 32], P(None, None, None, 'date', 'strip')
Inputs may be any that keep to these rules, and one draw needn't show every extreme that they name: `shifts`: zero at every chip of date ref_dates[t] in tile t. `ref_dates`: the reference dates of consecutive tiles lie in different blocks of 2 dates.
All inputs are finite; a program needn't handle non-finite values.
Results may differ from a plain program's by a relative error of at most 0.0021.
Values may be sent and summed in bfloat16 or wider, within the bound.
A program may use at most 64 MiB of HBM per device.

v0:
```python
import functools

import jax
import jax.numpy as jnp
from jax import lax
from jax.experimental import pallas as pl
from jax.experimental.pallas import tpu as pltpu
from jax.sharding import PartitionSpec as P

TILE_COUNT = 2
CHIP_SIZE = 64
TAP_COUNT = 8
SUBSTEPS = 64
LOOK_AZ = 5
LOOK_RG = 20
MARGIN = 12
LANES = 128
GROUP = 8

epsilon = 1e-06
MESH = pl.DeviceIdType.MESH


def tap_weights(k, fraction):
    distance = k.astype(jnp.float32) - (TAP_COUNT // 2 - 1) - fraction.astype(jnp.float32) / SUBSTEPS
    angle = jnp.pi * distance
    sinc = jnp.where(
        distance == 0.0, 1.0, jnp.sin(angle) / jnp.where(distance == 0.0, 1.0, angle)
    )
    weights = sinc * (0.5 + 0.5 * jnp.cos(jnp.pi * distance / (TAP_COUNT // 2)))
    weights = jnp.where((k >= 0) & (k < TAP_COUNT), weights, 0.0)
    return weights / jnp.sum(weights, axis=1, keepdims=True)


def spread_rows(row, count):
    tall = jnp.broadcast_to(row, (count, LANES))
    return pltpu.roll(tall, 0, 1, stride=1, stride_axis=0)


def split_dot(values, selector):
    high = values.astype(jnp.bfloat16)
    low = (values - high.astype(jnp.float32)).astype(jnp.bfloat16)
    return jnp.dot(high, selector, preferred_element_type=jnp.float32) + jnp.dot(
        low, selector, preferred_element_type=jnp.float32
    )


def kernel(
    n, strips, dims,
    frame_hbm, shifts_ref, fractions_ref, dates_ref,
    coh_ref, sums_ref,
    frame_ref, frame_sem, even_ref, odd_ref, lines_ref, cols_ref, cand_ref, edge_out, edge_in, picked, spots,
    series, sent, got, acc, part_buf, whole, looks, chip_rows, out_buf,
    ref_send, ref_recv, next_send, next_recv, coh_send, coh_recv, edge_send, edge_recv,
):
    tiles, chips_az, chips_rg, rows, cols = dims
    me = lax.axis_index("date")
    strip = lax.axis_index("strip")
    bits = n.bit_length() - 1
    groups = cand_ref.shape[1]
    all_rows = rows + 2 * MARGIN
    blocks = series.shape[3]
    wide = blocks * LANES
    kept_dates = series.shape[0] - 1
    images = frame_ref.shape[0]
    rest = cols - (blocks - 1) * LANES
    bf16 = jnp.bfloat16
    f32 = jnp.float32

    load = pltpu.make_async_copy(frame_hbm, frame_ref, frame_sem)
    load.start()
    barrier = pltpu.get_barrier_semaphore()
    for o in range(1, n):
        pl.semaphore_signal(
            barrier, inc=1, device_id={"date": lax.rem(me + o, n)}, device_id_type=MESH
        )
    has_low = strip > 0
    has_high = strip < strips - 1

    @pl.when(has_low)
    def _():
        pl.semaphore_signal(barrier, inc=1, device_id={"strip": strip - 1}, device_id_type=MESH)

    @pl.when(has_high)
    def _():
        pl.semaphore_signal(barrier, inc=1, device_id={"strip": strip + 1}, device_id_type=MESH)

    def for_rows(body):
        count = all_rows // CHIP_SIZE

        def step(i, carry):
            body(pl.multiple_of(i * CHIP_SIZE, CHIP_SIZE), CHIP_SIZE)
            return carry

        lax.fori_loop(0, count, step, 0)
        if all_rows > count * CHIP_SIZE:
            body(count * CHIP_SIZE, all_rows - count * CHIP_SIZE)

    def block_of(q, row, size, m):
        width = min(LANES, cols - m * LANES)
        value = frame_ref[q, pl.ds(row, size), m * LANES : m * LANES + width].astype(f32)
        if width < LANES:
            value = jnp.concatenate([value, jnp.zeros((size, LANES - width), f32)], axis=1)
        return value

    def pack_edges(row, size):
        at = lax.broadcasted_iota(jnp.int32, (size, LANES), 1)
        right = jnp.zeros((size, LANES), f32)
        left = jnp.zeros((size, LANES), f32)
        for q in range(images):
            place = (at >= MARGIN * q) & (at < MARGIN * (q + 1))
            last = block_of(q, row, size, blocks - 1)
            first = block_of(q, row, size, 0)
            last = pltpu.roll(last, (MARGIN * q - rest + MARGIN) % LANES, 1)
            if q:
                first = pltpu.roll(first, MARGIN * q, 1)
            right = jnp.where(place, last, right)
            left = jnp.where(place, first, left)
        edge_out[0, pl.ds(row, size), :] = right.astype(bf16)
        edge_out[1, pl.ds(row, size), :] = left.astype(bf16)

    load.wait()
    for_rows(pack_edges)

    def pick_tile(tc, carry):
        t = tc // 2
        gains = [
            jnp.where(dates_ref[t] == me * kept_dates + d, 1.0, 0.0).astype(f32)
            for d in range(kept_dates)
        ]

        def select(row, size):
            total = jnp.zeros((size, cols), f32)
            for d in range(kept_dates):
                image = frame_ref[d * tiles * 2 + tc, pl.ds(row, size), :]
                total = total + image.astype(f32) * gains[d]
            picked[pl.ds(row, size), :] = total

        for_rows(select)
        count = rows // GROUP
        for g in range(count):
            low = MARGIN + g * GROUP
            cand_ref[t, (tc % 2) * count + g] = picked[low : low + GROUP, :].astype(bf16)
        return carry

    lax.fori_loop(0, tiles * 2, pick_tile, 0)

    beside = jnp.minimum(strip, 1) + jnp.minimum(strips - 1 - strip, 1)
    pl.semaphore_wait(barrier, n - 1 + beside)

    edges = [
        pltpu.make_async_remote_copy(
            src_ref=edge_out.at[i], dst_ref=edge_in.at[i],
            send_sem=edge_send.at[i], recv_sem=edge_recv.at[i],
            device_id={"strip": strip + 1 - 2 * i}, device_id_type=MESH,
        )
        for i in range(2)
    ]

    @pl.when(has_high)
    def _():
        edges[0].start()

    @pl.when(has_low)
    def _():
        edges[1].start()

    orders = [list(range(bits))]
    for t in range(1, tiles):
        orders.append([0] + list(range(2, bits)) + [1] if bits > 2 else orders[0])
    offsets = []
    for order in orders:
        offset = [jnp.int32(0)]
        for s, b in enumerate(order):
            offset.append(offset[-1] + ((me // (1 << b)) % 2) * (groups >> (s + 1)))
        offsets.append(offset)

    def partner(b):
        return me + (1 - 2 * ((me // (1 << b)) % 2)) * (1 << b)

    def halving(t, s):
        b = orders[t][s]
        half = groups >> (s + 1)
        away = offsets[t][s] + (1 - (me // (1 << b)) % 2) * half
        source = cand_ref if s == 0 else acc
        return pltpu.make_async_remote_copy(
            src_ref=source.at[t, pl.ds(away, half)],
            dst_ref=part_buf.at[t, pl.ds(groups - 2 * half, half)],
            send_sem=ref_send.at[t, s],
            recv_sem=ref_recv.at[t, s],
            device_id={"date": partner(b)},
            device_id_type=MESH,
        )

    def add_half(t, s):
        half = groups >> (s + 1)
        source = cand_ref if s == 0 else acc
        target = whole if s == bits - 1 else acc
        at = pl.ds(offsets[t][s + 1], half)
        target[t, at] = source[t, at] + part_buf[t, groups - 2 * half : groups - half]

    def doubling(t, s):
        half = groups >> (s + 1)
        mine = whole.at[t, pl.ds(offsets[t][s + 1], half)]
        return pltpu.make_async_remote_copy(
            src_ref=mine,
            dst_ref=mine,
            send_sem=ref_send.at[t, bits + s],
            recv_sem=ref_recv.at[t, bits + s],
            device_id={"date": partner(orders[t][s])},
            device_id_type=MESH,
        )

    state = {"step": 0, "copies": None}

    def advance():
        step = state["step"]
        if step > 2 * bits:
            return
        sent_now = []
        for t in range(tiles):
            if step > 0:
                state["copies"][t].wait()
                if step <= bits:
                    add_half(t, step - 1)
            if step < bits:
                sent_now.append(halving(t, step))
                sent_now[-1].start()
            elif step < 2 * bits:
                sent_now.append(doubling(t, 2 * bits - 1 - step))
                sent_now[-1].start()
        state["copies"] = sent_now
        state["step"] = step + 1

    lane = lax.broadcasted_iota(jnp.int32, (LANES, LANES), 1)
    window = 96

    def resample(d, t, first, last):
        def chip_line(a, carry):
            row0 = pl.multiple_of(a * CHIP_SIZE, CHIP_SIZE)
            q = (d * tiles + t) * 2
            for m in range((chips_rg + 1) // 2):
                span = slice(m * LANES, (m + 1) * LANES)
                halves = []
                mats = []
                for side, src in ((0, even_ref), (1, odd_ref)):
                    r = 2 * m + side
                    if r >= chips_rg:
                        continue
                    row_at = ((d * tiles + t) * chips_az + a) * chips_rg + r
                    line_row = lines_ref[pl.ds(row_at, 1), :]
                    col_row = cols_ref[pl.ds(row_at, 1), :]
                    line_mat = spread_rows(line_row, CHIP_SIZE).astype(bf16)[:, :window]
                    col_mat = spread_rows(col_row, LANES)
                    keep = lane < CHIP_SIZE if side == 0 else lane >= CHIP_SIZE
                    mats.append(jnp.where(keep, col_mat, 0.0).astype(bf16))
                    both = jnp.concatenate(
                        [src[q, pl.ds(row0, window), span], src[q + 1, pl.ds(row0, window), span]],
                        axis=1,
                    )
                    halves.append(
                        jnp.dot(line_mat, both, preferred_element_type=f32).astype(bf16)
                    )
                re = jnp.concatenate([h[:, :LANES] for h in halves], axis=1)
                im = jnp.concatenate([h[:, LANES:] for h in halves], axis=1)
                stacked = jnp.concatenate([re, im], axis=0)
                matrix = jnp.concatenate(mats, axis=0)
                out = jnp.dot(stacked, matrix, preferred_element_type=f32).astype(bf16)
                for c in range(2):
                    piece = out[c * CHIP_SIZE : (c + 1) * CHIP_SIZE]
                    series[d, t, c, m, pl.ds(row0, CHIP_SIZE), :] = piece.astype(f32)
                    if d == 0:
                        sent[t, c, m, pl.ds(row0, CHIP_SIZE), :] = piece
            return carry

        lax.fori_loop(first, last, chip_line, 0)

    advance()

    chip = 0
    for d in range(kept_dates):
        for t in range(tiles):
            for a in range(chips_az):
                for r in range(chips_rg):
                    values = (
                        shifts_ref[0, d, t, a, r] + (MARGIN - TAP_COUNT // 2 + 1),
                        (r % 2) * CHIP_SIZE
                        - shifts_ref[1, d, t, a, r]
                        - (MARGIN - TAP_COUNT // 2 + 1),
                        fractions_ref[0, d, t, a, r],
                        fractions_ref[1, d, t, a, r],
                    )
                    for i, value in enumerate(values):
                        spots[i, chip : chip + 1, :] = jnp.full((1, LANES), value, jnp.int32)
                    chip += 1
    at = lax.broadcasted_iota(jnp.int32, (chip, LANES), 1)
    lines_ref[:chip] = tap_weights(at - spots[0, :chip], spots[2, :chip])
    cols_ref[:chip] = tap_weights((spots[1, :chip] - at) & (LANES - 1), spots[3, :chip])

    @pl.when(has_low)
    def _():
        edges[0].wait_recv()

    @pl.when(has_high)
    def _():
        edges[1].wait_recv()

    @pl.when(strip == 0)
    def _():
        edge_in[0] = jnp.zeros(edge_in.shape[1:], bf16)

    @pl.when(strip == strips - 1)
    def _():
        edge_in[1] = jnp.zeros(edge_in.shape[1:], bf16)

    advance()
    tall = even_ref.shape[1]

    def picker(depth, width, want):
        source = lax.broadcasted_iota(jnp.int32, (depth, width), 0)
        at = lax.broadcasted_iota(jnp.int32, (depth, width), 1)
        return jnp.where(source == want(at), 1.0, 0.0).astype(bf16)

    def moved(values, matrix):
        return jnp.dot(values, matrix, preferred_element_type=f32).astype(bf16)

    both_move = picker(
        2 * LANES,
        2 * LANES,
        lambda at: jnp.where(at < LANES, at + LANES - MARGIN, at - LANES + CHIP_SIZE - MARGIN),
    )
    first_move = picker(LANES, LANES, lambda at: at - MARGIN)
    row_cut = (all_rows // 2 + 15) // 16 * 16

    def shift_image(q, carry):
        low_move = picker(LANES, LANES, lambda at: jnp.where(at < MARGIN, at + MARGIN * q, -1))
        skip = rest + MARGIN
        high_move = picker(
            LANES,
            LANES,
            lambda at: jnp.where(
                (at >= skip) & (at < skip + MARGIN), at - skip + MARGIN * q, -1
            ),
        )
        for row, size in ((0, row_cut), (row_cut, all_rows - row_cut)):
            span = slice(row, row + size)
            even_ref[q, span, :LANES] = moved(frame_ref[q, span, :LANES], first_move) + moved(
                edge_in[0, span, :], low_move
            )
            for m in range(blocks - 1):
                width = min(2 * LANES, cols - m * LANES)
                pair = moved(
                    frame_ref[q, span, m * LANES : m * LANES + width], both_move[:width]
                )
                block = pair[:, :LANES]
                if m == blocks - 2:
                    block = block + moved(edge_in[1, span, :], high_move)
                even_ref[q, span, (m + 1) * LANES : (m + 2) * LANES] = block
                odd_ref[q, span, m * LANES : (m + 1) * LANES] = pair[:, LANES:]
        even_ref[q, all_rows:, :] = jnp.zeros((tall - all_rows, wide), bf16)
        odd_ref[q, all_rows:, :] = jnp.zeros((tall - all_rows, odd_ref.shape[2]), bf16)
        return carry

    lax.fori_loop(0, images, shift_image, 0)
    last_d = series.shape[0] - 2
    following = [None]
    for d in range(last_d + 1):
        for t in range(tiles):
            advance()
            resample(d, t, 0, chips_az)
            if d == 0 and t == tiles - 1:
                following[0] = pltpu.make_async_remote_copy(
                    src_ref=sent, dst_ref=got, send_sem=next_send, recv_sem=next_recv,
                    device_id={"date": lax.rem(me + n - 1, n)}, device_id_type=MESH,
                )

                @pl.when(me > 0)
                def _():
                    following[0].start()

    @pl.when(me < n - 1)
    def _():
        following[0].wait_recv()

        def body(i, carry):
            row = pl.multiple_of(i * 16, 16)
            for t in range(tiles):
                for c in range(2):
                    for m in range(blocks):
                        series[last_d + 1, t, c, m, pl.ds(row, 16), :] = got[
                            t, c, m, pl.ds(row, 16), :
                        ].astype(f32)
            return carry

        lax.fori_loop(0, rows // 16, body, 0)

    @pl.when(me == n - 1)
    def _():
        series[last_d + 1] = jnp.zeros(series.shape[1:], f32)

    advance()
    dates = series.shape[0]
    pairs = dates - 1
    look_rows = rows // LOOK_AZ
    for t in range(tiles):
        def look_block(y, carry):
            def add(total, value):
                return value if total is None else total + value

            row = pl.multiple_of(y * GROUP, GROUP)
            for m in range(blocks):
                span = slice(m * LANES, (m + 1) * LANES)
                power = [None] * dates
                cross = [[None, None] for _ in range(pairs)]
                for s in range(LOOK_AZ):
                    lines_at = pl.ds(y * (GROUP * LOOK_AZ) + s, GROUP, stride=LOOK_AZ)
                    here = [
                        [series[d, t, c, m, lines_at, :] for c in range(2)] for d in range(dates)
                    ]
                    for d in range(dates):
                        re, im = here[d]
                        power[d] = add(power[d], re * re + im * im)
                    for p in range(pairs):
                        ar, ai = here[p]
                        br, bi = here[p + 1]
                        cross[p][0] = add(cross[p][0], ar * br + ai * bi)
                        cross[p][1] = add(cross[p][1], ai * br - ar * bi)
                for d in range(dates):
                    looks[t, d, pl.ds(row, GROUP), span] = power[d]
                for p in range(pairs):
                    for c in range(2):
                        looks[t, dates + 2 * p + c, pl.ds(row, GROUP), span] = cross[p][c]
            return carry

        lax.fori_loop(0, look_rows // GROUP, look_block, 0)
        advance()

    looks_rg = cols // LOOK_RG
    col_id = lax.broadcasted_iota(jnp.int32, (wide, LANES), 0)
    lane_id = lax.broadcasted_iota(jnp.int32, (wide, LANES), 1)
    base = col_id - LOOK_RG * lane_id

    def selector(q):
        shifted = base + LOOK_RG * looks_rg * q
        hit = (shifted >= 0) & (shifted < LOOK_RG) & (col_id < cols)
        return jnp.where(hit, 1.0, 0.0).astype(f32)

    numer = jnp.zeros((look_rows, LANES), f32)
    early = jnp.zeros((look_rows, LANES), f32)
    later = jnp.zeros((look_rows, LANES), f32)
    for p in range(pairs):
        for t in range(tiles):
            picks = [selector((c * pairs + p) * tiles + t) for c in range(2)]
            for c in range(2):
                numer = numer + split_dot(looks[t, dates + 2 * p + c], picks[c].astype(bf16))
            pick = (picks[0] + picks[1]).astype(bf16)
            early = early + split_dot(looks[t, p], pick)
            later = later + split_dot(looks[t, p + 1], pick)
    coherence = numer / jnp.sqrt((early + epsilon) * (later + epsilon))
    share = look_rows // n
    for j in range(n):
        out_buf[j] = coherence[j * share : (j + 1) * share]
    coh_ref[me] = out_buf[me]
    copies = []
    for o in range(1, n):
        peer = lax.rem(me + o, n)
        copy = pltpu.make_async_remote_copy(
            src_ref=out_buf.at[peer], dst_ref=coh_ref.at[me],
            send_sem=coh_send.at[o], recv_sem=coh_recv.at[o],
            device_id={"date": peer}, device_id_type=MESH,
        )
        copy.start()
        copies.append(copy)
    while state["step"] <= 2 * bits:
        advance()

    line_groups = CHIP_SIZE // GROUP
    kept = dates - 1
    for t in range(tiles):
        def corr_line(a, carry):
            for m in range(blocks):
                low = m * LANES
                size = min(LANES, cols - low)
                span = slice(low, low + size)
                total = [jnp.zeros((GROUP, size), f32)] * (1 + 3 * kept)
                for g in range(line_groups):
                    at = a * line_groups + g
                    rr = whole[t, at, :, span].astype(f32)
                    ri = whole[t, rows // GROUP + at, :, span].astype(f32)
                    total[0] = total[0] + (rr * rr + ri * ri)
                    row = pl.multiple_of(at * GROUP, GROUP)
                    for d in range(kept):
                        sr = series[d, t, 0, m, pl.ds(row, GROUP), :size]
                        si = series[d, t, 1, m, pl.ds(row, GROUP), :size]
                        total[1 + 3 * d] = total[1 + 3 * d] + (rr * sr + ri * si)
                        total[2 + 3 * d] = total[2 + 3 * d] + (ri * sr - rr * si)
                        total[3 + 3 * d] = total[3 + 3 * d] + (sr * sr + si * si)
                for k in range(1 + 3 * kept):
                    chip_rows[t, a, k : k + 1, span] = jnp.sum(total[k], axis=0, keepdims=True)
            return carry

        lax.fori_loop(0, chips_az, corr_line, 0)
    col_id = lax.broadcasted_iota(jnp.int32, (cols, LANES), 0)
    lane_id = lax.broadcasted_iota(jnp.int32, (cols, LANES), 1)
    gap = col_id - CHIP_SIZE * lane_id
    pick = jnp.where((gap >= 0) & (gap < CHIP_SIZE), 1.0, 0.0).astype(bf16)
    for t in range(tiles):
        for a in range(chips_az):
            sums_ref[t, a] = split_dot(chip_rows[t, a], pick)

    for o in range(1, n):
        copies[o - 1].wait()

    @pl.when(me > 0)
    def _():
        following[0].wait_send()

    @pl.when(has_high)
    def _():
        edges[0].wait_send()

    @pl.when(has_low)
    def _():
        edges[1].wait_send()


def per_device(n, strips, acquisitions, shifts, fractions, ref_dates):
    dates_local, tiles, _, all_rows, cols = acquisitions.shape
    rows = all_rows - 2 * MARGIN
    chips_az, chips_rg = shifts.shape[3:]
    blocks = -(-cols // LANES)
    wide = blocks * LANES
    images = dates_local * tiles * 2
    frames = acquisitions.reshape(images, all_rows, cols)
    tall = -(-all_rows // 32) * 32
    odd_wide = (chips_rg // 2) * LANES
    chips = dates_local * tiles * chips_az * chips_rg
    chips_tall = -(-chips // GROUP) * GROUP
    groups = -(-(2 * rows // GROUP) // n) * n

    look_rows = rows // LOOK_AZ
    looks_rg = cols // LOOK_RG
    share = look_rows // n
    stat_rows = 1 + 3 * dates_local
    bits = n.bit_length() - 1
    vmem = pl.BlockSpec(memory_space=pltpu.VMEM)
    f32 = jnp.float32
    bf16 = jnp.bfloat16
    dma = pltpu.SemaphoreType.DMA
    coh, sums = pl.pallas_call(
        functools.partial(kernel, n, strips, (tiles, chips_az, chips_rg, rows, cols)),
        out_shape=(
            jax.ShapeDtypeStruct((n, share, LANES), f32),
            jax.ShapeDtypeStruct((tiles, chips_az, stat_rows, LANES), f32),
        ),
        in_specs=[pl.BlockSpec(memory_space=pl.ANY)] + [pl.BlockSpec(memory_space=pltpu.SMEM)] * 3,
        out_specs=(vmem, vmem),
        scratch_shapes=[
            pltpu.VMEM((images, all_rows, cols), bf16),
            dma,
            pltpu.VMEM((images, tall, wide), bf16),
            pltpu.VMEM((images, tall, odd_wide), bf16),
            pltpu.VMEM((chips_tall, LANES), f32),
            pltpu.VMEM((chips_tall, LANES), f32),
            pltpu.VMEM((tiles, groups, GROUP, cols), bf16),
            pltpu.VMEM((2, all_rows, LANES), bf16),
            pltpu.VMEM((2, all_rows, LANES), bf16),
            pltpu.VMEM((all_rows, cols), f32),
            pltpu.VMEM((4, chips_tall, LANES), jnp.int32),
            pltpu.VMEM((dates_local + 1, tiles, 2, wide // LANES, rows, LANES), f32),
            pltpu.VMEM((tiles, 2, wide // LANES, rows, LANES), bf16),
            pltpu.VMEM((tiles, 2, wide // LANES, rows, LANES), bf16),
            pltpu.VMEM((tiles, groups, GROUP, cols), bf16),
            pltpu.VMEM((tiles, groups, GROUP, cols), bf16),
            pltpu.VMEM((tiles, groups, GROUP, cols), bf16),
            pltpu.VMEM((tiles, dates_local + 1 + 2 * dates_local, look_rows, wide), f32),
            pltpu.VMEM((tiles, chips_az, stat_rows, cols), f32),
            pltpu.VMEM((n, share, LANES), f32),
            dma((tiles, 2 * bits)), dma((tiles, 2 * bits)), dma, dma, dma((n,)), dma((n,)),
            dma((2,)), dma((2,)),
        ],
        compiler_params=pltpu.CompilerParams(
            collective_id=0, has_side_effects=True, vmem_limit_bytes=50 * 1024 * 1024
        ),
    )(frames, shifts, fractions, ref_dates)

    stats = sums[..., :chips_rg]
    ref_power = stats[:, :, 0]
    sec = stats[:, :, 1:].reshape(tiles, chips_az, dates_local, 3, chips_rg)
    sec = sec.transpose(3, 2, 0, 1, 4)
    denominator = jnp.sqrt((ref_power[None] + epsilon) * (sec[2] + epsilon))
    chip_corr = sec[:2] / denominator[None]
    looked = coh.reshape(n, share, 2, dates_local, tiles, looks_rg)
    looked = looked.transpose(2, 0, 3, 4, 1, 5).reshape(2, n * dates_local, tiles, share, looks_rg)
    return (chip_corr, looked[:, : n * dates_local - 1])


def solution(mesh):
    return jax.shard_map(
        functools.partial(per_device, mesh.shape["date"], mesh.shape["strip"]),
        mesh=mesh,
        in_specs=(
            P("date", None, None, None, "strip"),
            P(None, "date", None, None, "strip"),
            P(None, "date", None, None, "strip"),
            P(),
        ),
        out_specs=(P(None, "date", None, None, "strip"), P(None, None, None, "date", "strip")),
        check_vma=False,
    )
```

profile of v0, /device:TPU:0, one launch (start us, length us, event | category | flops | bytes accessed | tf_op | source)
XLA Modules:
  0.0 59.2 jit_solution(359961452608288278)
XLA Ops:
  0.6 0.0 copy-start
  0.6 0.7 %copy.23.shifts_ref = s32[2,2,2,5,5]{4,3,2,1,0:T(8,128)S(1)} copy(s32[2,2,2,5,5]{4,2,3,1,0:T(2,128)} %param.5) | data formatting | bytes 1600 | tf_op args[1]
  1.4 0.7 %copy.24.fractions_ref = s32[2,2,2,5,5]{4,3,2,1,0:T(8,128)S(1)} copy(s32[2,2,2,5,5]{4,2,3,1,0:T(2,128)} %param.6) | data formatting | bytes 1600 | tf_op args[2]
  2.1 3.0 %copy.22 = bf16[2,2,2,344,320]{4,3,2,1,0:T(8,128)(2,1)S(1)} copy(bf16[2,2,2,344,320]{3,4,2,1,0:T(8,128)(2,1)} %param.4) | data formatting | bytes 3522560 | tf_op args[0]
  5.1 0.0 copy-done
  5.1 52.0 %shard_map.59 = (f32[16,4,128]{2,1,0:T(4,128)S(1)}, f32[2,5,7,128]{3,2,1,0:T(8,128)S(1)}) custom-call(bf16[8,344,320]{2,1,0:T(8,128)(2,1)S(1)} %bitcast.13, s32[2,2,2,5,5]{4,3,2,1,0:T(8,128)S(1)} %copy.23.shifts_ref, s32[2,2,2,5,5]{4,3,2,1,0:T(8,128)S(1)} %copy.24.fractions_ref, s32[2]{0:T(128)S(1)} %copy-done), custom_call_target="tpu_custom_call" | custom-call | tf_op jit(solution)/shard_map/pallas_call | solution.py:550
  57.2 0.6 %copy.31 = f32[2,2,2,5,5]{4,2,3,1,0:T(2,128)} copy(f32[2,2,2,5,5]{4,2,0,1,3:T(2,128)S(1)} %slice_divide_fusion) | data formatting | bytes 1600
  57.9 0.4 reshape.27
  58.2 0.1 copy.30
  58.4 0.8 %copy.32 = f32[2,31,2,4,16]{1,4,3,2,0:T(8,128)} copy(f32[2,31,2,4,16]{4,1,3,2,0:T(8,128)S(1)} %bitcast.14) | data formatting | bytes 63488
  (6 shorter events, 0.1 us)
Async XLA Ops:
  0.6 4.5 %copy-start = (s32[2]{0:T(128)S(1)}, s32[2]{0:T(128)}, u32[]{:S(2)}) copy-start(s32[2]{0:T(128)} %dates_ref.1) | copy-start | bytes 28
where the time goes:
time: 59.5 us; the launch traced here: 59.2 us
  Pallas kernels  52 us (87%)
  local copies, waits for them, and re-layouts  6.42 us (11%)
  between operations  0.73 us (1%)
    pallas_call x1, Pallas kernels, per_device(): pl.pallas_call(functools.partial(kernel, n, strips, (tiles, chips_az, chi...  52 us
    unnamed x7, local copies, waits for them, and re-layouts  5.87 us

commit v1 on v0

v1 whole, which is shorter than its diff:
```python
import functools

import jax
import jax.numpy as jnp
from jax import lax
from jax.experimental import pallas as pl
from jax.experimental.pallas import tpu as pltpu
from jax.sharding import PartitionSpec as P

CHIP_SIZE = 64
TAP_COUNT = 8
SUBSTEPS = 64
LOOK_AZ = 5
LOOK_RG = 20
MARGIN = 12
LANES = 128
GROUP = 8
PACK = 16
HALO = 16
WINDOW = 96
BAND = 160
CORES = 2
SIDES = 2

epsilon = 1e-06
MESH = pl.DeviceIdType.MESH


def tap_weights(k, fraction):
    distance = k.astype(jnp.float32) - (TAP_COUNT // 2 - 1) - fraction.astype(jnp.float32) / SUBSTEPS
    angle = jnp.pi * distance
    sinc = jnp.where(
        distance == 0.0, 1.0, jnp.sin(angle) / jnp.where(distance == 0.0, 1.0, angle)
    )
    weights = sinc * (0.5 + 0.5 * jnp.cos(jnp.pi * distance / (TAP_COUNT // 2)))
    weights = jnp.where((k >= 0) & (k < TAP_COUNT), weights, 0.0)
    return weights / jnp.sum(weights, axis=1, keepdims=True)


def spread(row, count, start):
    tall = jnp.broadcast_to(row, (count, LANES))
    return pltpu.roll(tall, start, 1, stride=1, stride_axis=0)


def split_dot(values, selector):
    high = values.astype(jnp.bfloat16)
    low = (values - high.astype(jnp.float32)).astype(jnp.bfloat16)
    return jnp.dot(high, selector, preferred_element_type=jnp.float32) + jnp.dot(
        low, selector, preferred_element_type=jnp.float32
    )


def kernel(
    n, strips, dims,
    frame_hbm, shifts_hbm, fractions_hbm, dates_hbm,
    coh_ref, corr_ref,
    frame, shifts_ref, fractions_ref, dates_ref, spots, line_base, col_base,
    cand, core_in, y_out, y_in, z_out, z_in, whole,
    series, sent, got, cross_sums, powers, selectors, out_buf, coh_in, ordered, totals,
    load_sem, small_sem, edge_send, edge_recv, core_send, core_recv, y_send, y_recv,
    z_send, z_recv, next_send, next_recv, coh_send, coh_recv,
):
    tiles, kept, chips_az, chips_rg, rows, cols = dims
    me = lax.axis_index("date")
    strip = lax.axis_index("strip")
    core = me % CORES
    side = (me // CORES) % SIDES
    levels = n // (CORES * SIDES)
    level = me // (CORES * SIDES)
    bf16 = jnp.bfloat16
    f32 = jnp.float32
    chips = chips_az * chips_rg
    chip_units = CHIP_SIZE // PACK
    half_chips = -(-chips // SIDES)
    half_units = whole.shape[2]
    piece = half_units // levels
    steps = [levels // 2] + [o for o in range(1, levels) if o != levels // 2]

    def at_level(o):
        return lax.rem(level + o, levels)

    def device(z, y, c):
        return {"date": (z * SIDES + y) * CORES + c}

    def remote(src, dst, send, recv, where):
        return pltpu.make_async_remote_copy(
            src_ref=src, dst_ref=dst, send_sem=send, recv_sem=recv,
            device_id=where, device_id_type=MESH,
        )

    inner = pl.ds(HALO, cols)
    loads = {}
    for i, (d, t) in enumerate(((core, 1 - core), (1 - core, 1 - core), (core, core), (1 - core, core))):
        loads[i] = pltpu.make_async_copy(
            frame_hbm.at[d, t], frame.at[d, t, :, inner, :], load_sem.at[i]
        )
        loads[i].start()
    smalls = [
        pltpu.make_async_copy(src, dst, small_sem.at[i])
        for i, (src, dst) in enumerate(
            ((shifts_hbm, shifts_ref), (fractions_hbm, fractions_ref), (dates_hbm, dates_ref))
        )
    ]
    for copy in smalls:
        copy.start()

    barrier = pltpu.get_barrier_semaphore()
    for o in range(1, n):
        pl.semaphore_signal(
            barrier, inc=1, device_id={"date": lax.rem(me + o, n)}, device_id_type=MESH
        )
    has_low = strip > 0
    has_high = strip < strips - 1

    @pl.when(has_low)
    def _():
        pl.semaphore_signal(barrier, inc=1, device_id={"strip": strip - 1}, device_id_type=MESH)

    @pl.when(has_high)
    def _():
        pl.semaphore_signal(barrier, inc=1, device_id={"strip": strip + 1}, device_id_type=MESH)

    edge_zero = jnp.zeros((kept, tiles, 2, HALO, frame.shape[4]), bf16)

    @pl.when(strip == 0)
    def _():
        frame[:, :, :, 0:HALO, :] = edge_zero

    @pl.when(strip == strips - 1)
    def _():
        frame[:, :, :, HALO + cols : 2 * HALO + cols, :] = edge_zero

    lane = lax.broadcasted_iota(jnp.int32, (GROUP, LANES), 1)

    def wide(count):
        return lax.broadcasted_iota(jnp.int32, (count, LANES), 1)

    for copy in smalls:
        copy.wait()

    for d in range(kept):
        for a in range(chips_az):
            row = (d * chips_az + a) * tiles
            for i in range(2):
                spots[i, row : row + tiles, :chips_rg] = shifts_ref[i, d, a]
                spots[2 + i, row : row + tiles, :chips_rg] = fractions_ref[i, d, a]
    spot_rows = kept * chips_az * tiles
    first_tap = MARGIN - TAP_COUNT // 2 + 1
    at = wide(spot_rows)
    for r in range(chips_rg):
        values = [
            jnp.broadcast_to(spots[i, 0:spot_rows, r : r + 1], (spot_rows, LANES)) for i in range(4)
        ]
        line_tap = ((LANES - at) & (LANES - 1)) - (values[0] + first_tap)
        line_base[r, 0:spot_rows, :] = tap_weights(line_tap, values[2])
        col_tap = at - (values[1] + (first_tap + HALO - MARGIN))
        col_base[r, 0:spot_rows, :] = tap_weights(col_tap, values[3])

    for y in range(SIDES):
        used = (min(chips, (y + 1) * half_chips) - y * half_chips) * chip_units
        if used < half_units:
            for t in range(tiles):
                cand[t, y, used:half_units] = jnp.zeros((half_units - used, PACK, LANES), bf16)

    dates_row = dates_ref[0:1, :]

    def pick(t):
        def body(r, carry):
            at = wide(CHIP_SIZE)
            low = at < CHIP_SIZE
            inside = at >= MARGIN
            date_lane = lax.broadcasted_iota(jnp.int32, (1, tiles), 1)
            date = jnp.sum(jnp.where(date_lane == t, dates_row, 0), axis=1, keepdims=True)
            here = pl.ds(pl.multiple_of(HALO + r * CHIP_SIZE, PACK), CHIP_SIZE)
            parts = []
            for c in range(2):
                total = None
                for d in range(kept):
                    gain = jnp.where(date == me * kept + d, 1.0, 0.0).astype(f32)
                    value = frame[d, t, c, here, :].astype(f32) * gain
                    total = value if total is None else total + value
                blocks = []
                for b in range(-(-total.shape[1] // LANES)):
                    block = total[:, b * LANES : min((b + 1) * LANES, total.shape[1])]
                    if block.shape[1] < LANES:
                        block = jnp.concatenate(
                            [block, jnp.zeros((CHIP_SIZE, LANES - block.shape[1]), f32)], axis=1
                        )
                    blocks.append(block)
                parts.append(blocks)
            for a in range(chips_az):
                b = a // 2
                moves = (LANES - MARGIN, CHIP_SIZE - MARGIN)
                pair = [p[b] for p in parts]
                if a % 2:
                    moves = moves[::-1]
                    pair = [jnp.where(inside, p[b], p[b + 1]) for p in parts]
                pair = [pltpu.roll(v, m, 1) for v, m in zip(pair, moves)]
                mixed = jnp.where(low, pair[0], pair[1]).astype(bf16)
                chip = a * chips_rg + r
                unit = (chip % half_chips) * chip_units
                cand[t, chip // half_chips, pl.ds(unit, chip_units)] = mixed.reshape(
                    chip_units, PACK, LANES
                )
            return carry

        lax.fori_loop(0, chips_rg, body, 0)

    loads[0].wait()
    loads[1].wait()
    pick(1 - core)

    beside = jnp.minimum(strip, 1) + jnp.minimum(strips - 1 - strip, 1)
    pl.semaphore_wait(barrier, n - 1 + beside)

    core_rs = [
        remote(cand.at[1 - core, y], core_in.at[y], core_send.at[i], core_recv.at[i],
               device(level, side, 1 - core))
        for i, y in enumerate((1 - side, side))
    ]
    for copy in core_rs:
        copy.start()

    order = ((core, core), (1 - core, 1 - core), (core, 1 - core), (1 - core, core))
    edges = []
    for i, (d, t) in enumerate(order):
        up = remote(
            frame_hbm.at[d, t, :, pl.ds(cols - HALO, HALO), :], frame.at[d, t, :, pl.ds(0, HALO), :],
            edge_send.at[0, i], edge_recv.at[0, i], {"strip": strip + 1},
        )
        down = remote(
            frame_hbm.at[d, t, :, pl.ds(0, HALO), :], frame.at[d, t, :, pl.ds(HALO + cols, HALO), :],
            edge_send.at[1, i], edge_recv.at[1, i], {"strip": strip - 1},
        )
        edges.append((up, down))

        @pl.when(has_high)
        def _():
            up.start()

        @pl.when(has_low)
        def _():
            down.start()

    def edge_wait(i):
        @pl.when(has_low)
        def _():
            edges[i][0].wait_recv()

        @pl.when(has_high)
        def _():
            edges[i][1].wait_recv()

    loads[2].wait()
    loads[3].wait()
    pick(core)

    def level_piece(z):
        return pl.ds(z * piece, piece)

    y_rs = [
        remote(y_out.at[level_piece(at_level(o))], y_in.at[k], y_send.at[0, k], y_recv.at[0, k],
               device(level, 1 - side, core))
        for k, o in enumerate(steps + [0])
    ]
    z_rs = [
        remote(z_out.at[k], z_in.at[k], z_send.at[0, k], z_recv.at[0, k],
               device(at_level(o), side, core))
        for k, o in enumerate(steps)
    ]
    mine = whole.at[core, side, level_piece(level)]
    z_ag = [
        remote(mine, mine, z_send.at[1, k], z_recv.at[1, k], device(at_level(o), side, core))
        for k, o in enumerate(steps)
    ]
    y_ag = []
    for k, o in enumerate(steps + [0]):
        part = whole.at[core, side, level_piece(at_level(levels - o))]
        y_ag.append(
            remote(part, part, y_send.at[1, k], y_recv.at[1, k], device(level, 1 - side, core))
        )
    core_ag = [
        remote(whole.at[core, y], whole.at[core, y], core_send.at[2 + i], core_recv.at[2 + i],
               device(level, side, 1 - core))
        for i, y in enumerate((side, 1 - side))
    ]

    def ref_core():
        core_rs[0].wait_recv()
        y_out[...] = cand[core, 1 - side] + core_in[1 - side]
        for copy in y_rs:
            copy.start()

    def piece_sum(k, o):
        at = level_piece(at_level(o))
        y_rs[k].wait_recv()
        return cand[core, side, at] + core_in[side, at] + y_in[k]

    def ref_side(k):
        if k == 0:
            core_rs[1].wait_recv()
        z_out[k] = piece_sum(k, steps[k])
        z_rs[k].start()

    def ref_level():
        total = piece_sum(len(steps), 0)
        for k in range(len(steps)):
            z_rs[k].wait_recv()
            total = total + z_in[k]
        whole[core, side, level_piece(level)] = total
        for copy in z_ag:
            copy.start()
        y_ag[len(steps)].start()

    def ref_back(k):
        z_ag[k].wait_recv()
        y_ag[k].start()
        if k == len(steps) - 1:
            core_ag[0].start()

    def ref_other():
        for copy in y_ag:
            copy.wait_recv()
        core_ag[1].start()

    low_lane = wide(CHIP_SIZE) < CHIP_SIZE

    def halves(count):
        return wide(count) < CHIP_SIZE

    def chip_column(d, t, r, slot):
        row0 = pl.multiple_of(r * CHIP_SIZE, CHIP_SIZE)
        window = pl.ds(row0, WINDOW)

        def base(ref, a):
            return ref[r, pl.ds((d * chips_az + a) * tiles + t, 1), :]

        partial = [None] * chips_az
        reach = CHIP_SIZE + 2 * MARGIN
        for a in range(0, chips_az - 1, 2):
            b = a // 2
            span = slice(b * LANES, b * LANES + BAND)
            image = jnp.concatenate([frame[d, t, c, window, span] for c in range(2)], axis=0)
            first = spread(base(line_base, a), reach, 0)
            second = spread(base(line_base, a + 1), BAND - CHIP_SIZE, CHIP_SIZE)
            shared = reach - CHIP_SIZE
            matrix = jnp.concatenate(
                [
                    jnp.where(halves(CHIP_SIZE), first[:CHIP_SIZE], 0.0),
                    jnp.where(halves(shared), first[CHIP_SIZE:], second[:shared]),
                    jnp.where(halves(BAND - reach), 0.0, second[shared:]),
                ],
                axis=0,
            ).astype(bf16)
            out = jnp.dot(image, matrix, preferred_element_type=f32)
            re, im = out[:WINDOW], out[WINDOW:]
            left = halves(WINDOW)
            partial[a] = jnp.where(left, re, pltpu.roll(im, CHIP_SIZE, 1)).astype(bf16)
            partial[a + 1] = jnp.where(left, pltpu.roll(re, CHIP_SIZE, 1), im).astype(bf16)
        if chips_az % 2:
            a = chips_az - 1
            span = slice(a * CHIP_SIZE, a * CHIP_SIZE + reach)
            row = base(line_base, a)
            left = halves(reach)
            top = jnp.where(left, spread(row, reach, 0), 0.0).astype(bf16)
            bottom = jnp.where(left, 0.0, spread(row, reach, CHIP_SIZE)).astype(bf16)
            partial[a] = (
                jnp.dot(frame[d, t, 0, window, span], top, preferred_element_type=f32)
                + jnp.dot(frame[d, t, 1, window, span], bottom, preferred_element_type=f32)
            ).astype(bf16)
        for a in range(chips_az):
            matrix = spread(base(col_base, a), CHIP_SIZE, 0)[:, :WINDOW].astype(bf16)
            out = jnp.dot(matrix, partial[a], preferred_element_type=f32).astype(bf16)
            if slot is not None:
                unit = (a * chips_rg + r) * chip_units
                sent[slot, pl.ds(unit, chip_units)] = out.reshape(chip_units, PACK, LANES)
            out = out.astype(f32)
            series[t, d + t, a, pl.ds(row0, CHIP_SIZE), :] = out
            power = jnp.sum((out * out).reshape(GROUP, GROUP, LANES), axis=0)
            totals[1 + 2 * kept + d, r, pl.ds((a * tiles + t) * GROUP, GROUP), :] = power

    def resample(i, first, last):
        d, t = order[i]

        def body(j, carry):
            chip_column(d, t, lax.rem(j + 1, chips_rg), i if i < 2 else None)
            return carry

        lax.fori_loop(first, last, body, 0)

    inside_cols = chips_rg - 2
    peer = me + 2 * core - 1
    has_peer = (peer >= 0) & (peer < n)
    outward = remote(sent.at[0], got.at[0], next_send.at[0], next_recv.at[0], {"date": peer})
    inward = remote(
        sent.at[1], got.at[1], next_send.at[1], next_recv.at[1], device(level, side, 1 - core)
    )

    resample(0, 0, 1)
    ref_core()
    resample(0, 1, inside_cols)
    edge_wait(0)
    resample(0, inside_cols, chips_rg)

    @pl.when(has_peer)
    def _():
        outward.start()

    ref_side(0)
    resample(1, 0, inside_cols)
    edge_wait(1)
    resample(1, inside_cols, chips_rg)
    inward.start()
    ref_side(1)
    edge_wait(2)
    resample(2, 0, chips_rg)
    for k in range(2, len(steps)):
        ref_side(k)
    edge_wait(3)
    resample(3, 0, chips_rg)

    looks_rg = cols // LOOK_RG
    look_rows = rows // LOOK_AZ

    def pick_rows(t, pos, a, s):
        return series[t, pos, a, pl.ds(s, looks_rg, stride=LOOK_RG), :]

    def look(t, early, wanted):
        def body(a, carry):
            sums = [jnp.zeros((looks_rg, LANES), f32) for _ in range(2 + len(wanted))]
            for s in range(LOOK_RG):
                first = pick_rows(t, early, a, s)
                second = pick_rows(t, early + 1, a, s)
                sums[0] = sums[0] + first * second
                sums[1] = sums[1] + first * pltpu.roll(second, CHIP_SIZE, 1)
                for i, pos in enumerate(wanted):
                    value = pick_rows(t, pos, a, s)
                    sums[2 + i] = sums[2 + i] + value * value
            span = pl.ds(pl.multiple_of(a * LANES, LANES), LANES)
            row = pl.multiple_of((early * tiles + t) * looks_rg, GROUP)
            for c in range(2):
                cross_sums[c, pl.ds(row, looks_rg), span] = sums[c]
            for i, pos in enumerate(wanted):
                row = pl.multiple_of((pos * tiles + t) * looks_rg, GROUP)
                powers[pl.ds(row, looks_rg), span] = sums[2 + i]
            return carry

        lax.fori_loop(0, chips_az, body, 0)

    def unpack(i, t, pos):
        def body(j, carry):
            for a in range(chips_az):
                unit = a * chips_rg * chip_units + j * chip_units
                value = got[i, pl.ds(unit, chip_units)].reshape(CHIP_SIZE, LANES)
                row = pl.multiple_of(j * CHIP_SIZE, CHIP_SIZE)
                series[t, pos, a, pl.ds(row, CHIP_SIZE), :] = value.astype(f32)
            return carry

        lax.fori_loop(0, chips_rg, body, 0)

    look(0, 0, (0, 1))
    look(1, 1, (1, 2))

    def build_selectors(a, carry):
        line = lax.broadcasted_iota(jnp.int32, (LANES, LANES), 0)
        y = lax.broadcasted_iota(jnp.int32, (LANES, LANES), 1)
        gap = a * CHIP_SIZE + (line & (CHIP_SIZE - 1)) - LOOK_AZ * y
        hit = (gap >= 0) & (gap < LOOK_AZ)
        span = pl.ds(pl.multiple_of(a * LANES, LANES), LANES)
        selectors[0, span, :] = jnp.where(hit, 1.0, 0.0).astype(bf16)
        selectors[1, span, :] = jnp.where(
            hit, jnp.where(line < CHIP_SIZE, -1.0, 1.0), 0.0
        ).astype(bf16)
        return carry

    lax.fori_loop(0, chips_az, build_selectors, 0)

    inward.wait_recv()
    unpack(1, core, 2 * (1 - core))
    look(core, 1 - core, (2 * (1 - core),))
    ref_level()

    @pl.when(has_peer)
    def _():
        outward.wait_recv()
        unpack(0, 1 - core, 2 * core)

    @pl.when(jnp.logical_not(has_peer))
    def _():
        series[1 - core, 2 * core] = jnp.zeros(series.shape[2:], f32)

    look(1 - core, core, (2 * core,))

    summed = [split_dot(cross_sums[c], selectors[c]) for c in range(2)]
    power = split_dot(powers[...], selectors[0])
    count = kept * tiles * looks_rg
    skip = tiles * looks_rg
    scale = jnp.sqrt((power[:count] + epsilon) * (power[skip : skip + count] + epsilon))
    coherence = jnp.concatenate([v / scale for v in summed], axis=0).T
    share = look_rows // n
    for j in range(n):
        out_buf[j] = coherence[j * share : (j + 1) * share]
    coh_in[me] = out_buf[me]
    relays = []
    for o in range(1, n):
        to = lax.rem(me + o, n)
        copy = remote(
            out_buf.at[to], coh_in.at[me], coh_send.at[o], coh_recv.at[o], {"date": to}
        )
        copy.start()
        relays.append(copy)

    for k in range(len(steps)):
        ref_back(k)

    def correlate(t, y):
        def body(j, carry):
            chip = y * half_chips + j
            a = chip // chips_rg
            r = chip % chips_rg
            ref = whole[t, y, pl.ds(j * chip_units, chip_units)]
            ref = ref.reshape(CHIP_SIZE, LANES).astype(f32)
            turned = pltpu.roll(ref, CHIP_SIZE, 1)
            row = pl.multiple_of(r * CHIP_SIZE, CHIP_SIZE)
            to = pl.ds(pl.multiple_of((a * tiles + t) * GROUP, GROUP), GROUP)

            def put(k, value):
                total = jnp.sum(value.reshape(GROUP, GROUP, LANES), axis=0)
                totals[k, r, to, :] = total

            put(0, ref * ref)
            for d in range(kept):
                value = series[t, d + t, a, pl.ds(row, CHIP_SIZE), :]
                put(1 + 2 * d, ref * value)
                put(2 + 2 * d, turned * value)
            return carry

        lax.fori_loop(0, jnp.minimum(half_chips, chips - y * half_chips), body, 0)

    correlate(core, side)
    ref_other()
    correlate(core, 1 - side)
    core_ag[0].wait_recv()
    correlate(1 - core, side)
    core_ag[1].wait_recv()
    correlate(1 - core, 1 - side)

    kinds = totals.shape[0]
    group_rows = totals.shape[2] // GROUP
    lane16 = wide(group_rows)
    sign = jnp.where(lane16 < CHIP_SIZE, 1.0, -1.0).astype(f32)
    folded = []
    for k in range(kinds):
        line = []
        for r in range(chips_rg):
            total = None
            for s in range(GROUP):
                value = totals[k, r, pl.ds(s, group_rows, stride=GROUP), :]
                total = value if total is None else total + value
            if 1 <= k <= 2 * kept and k % 2 == 0:
                total = total * sign
            line.append(total)
        folded.append(jnp.concatenate(line, axis=1))
    folded = jnp.concatenate(folded, axis=0)
    depth = chips_rg * LANES
    source = lax.broadcasted_iota(jnp.int32, (depth, LANES), 0)
    target = lax.broadcasted_iota(jnp.int32, (depth, LANES), 1)
    gap = source - target * LANES
    gather = jnp.where((gap >= 0) & (gap < LANES), 1.0, 0.0).astype(bf16)
    sums = split_dot(folded, gather)
    sums = [sums[k * group_rows : (k + 1) * group_rows] for k in range(kinds)]
    for d in range(kept):
        scale = jnp.sqrt((sums[0] + epsilon) * (sums[1 + 2 * kept + d] + epsilon))
        for c in range(2):
            value = sums[1 + 2 * d + c] / scale
            for a in range(chips_az):
                corr_ref[c, d, a] = value[a * tiles : (a + 1) * tiles, :chips_rg]

    for copy in relays:
        copy.wait_recv()
    pairs = n * kept
    lane_n = wide(n)
    for y in range(share):
        value = coh_in[:, y, :]
        ordered[y, pl.ds(0, n, stride=2), :] = value
        ordered[y, pl.ds(1, n, stride=2), :] = pltpu.roll(value, LANES - tiles * looks_rg, 1)
    lane_p = wide(pairs)
    for y in range(share):
        first = (lane_p & (2 * looks_rg - 1)) < looks_rg
        value = jnp.where(first, ordered[y, 0:pairs, :], ordered[y, 1 : pairs + 1, :]).T
        for c in range(2):
            for t in range(tiles):
                row = c * kept * tiles * looks_rg + t * looks_rg
                coh_ref[c, t, y] = value[row : row + looks_rg, : pairs - 1]

    for copy in relays + core_rs + y_rs + z_rs + z_ag + y_ag + core_ag + [inward]:
        copy.wait_send()

    @pl.when(has_peer)
    def _():
        outward.wait_send()

    for up, down in edges:
        @pl.when(has_high)
        def _():
            up.wait_send()

        @pl.when(has_low)
        def _():
            down.wait_send()


def per_device(n, strips, acquisitions, shifts, fractions, ref_dates):
    kept, tiles, _, all_rows, cols = acquisitions.shape
    rows = all_rows - 2 * MARGIN
    chips_az, chips_rg = shifts.shape[3:]
    chips = chips_az * chips_rg
    units = chips * CHIP_SIZE // PACK
    levels = n // (CORES * SIDES)
    half_chips = -(-chips // SIDES)
    piece = -(-(half_chips * CHIP_SIZE // PACK) // levels)
    half_units = piece * levels
    looks_rg = cols // LOOK_RG
    look_rows = rows // LOOK_AZ
    share = look_rows // n
    spot_rows = -(-(kept * chips_az * tiles) // GROUP) * GROUP
    group_rows = -(-(chips_az * tiles) // GROUP) * GROUP
    kinds = 1 + 3 * kept
    f32 = jnp.float32
    bf16 = jnp.bfloat16
    dma = pltpu.SemaphoreType.DMA
    vmem = pl.BlockSpec(memory_space=pltpu.VMEM)
    frames = jnp.swapaxes(acquisitions, 3, 4)
    order = (0, 1, 3, 2, 4)
    coh, corr = pl.pallas_call(
        functools.partial(kernel, n, strips, (tiles, kept, chips_az, chips_rg, rows, cols)),
        out_shape=(
            jax.ShapeDtypeStruct((2, tiles, share, looks_rg, n * kept - 1), f32),
            jax.ShapeDtypeStruct((2, kept, chips_az, tiles, chips_rg), f32),
        ),
        in_specs=[pl.BlockSpec(memory_space=pl.ANY)] * 4,
        out_specs=(vmem, vmem),
        scratch_shapes=[
            pltpu.VMEM((kept, tiles, 2, cols + 2 * HALO, all_rows), bf16),
            pltpu.VMEM((2, kept, chips_az, tiles, chips_rg), jnp.int32),
            pltpu.VMEM((2, kept, chips_az, tiles, chips_rg), jnp.int32),
            pltpu.VMEM((1, tiles), jnp.int32),
            pltpu.VMEM((4, spot_rows, LANES), jnp.int32),
            pltpu.VMEM((chips_rg, spot_rows, LANES), f32),
            pltpu.VMEM((chips_rg, spot_rows, LANES), f32),
            pltpu.VMEM((tiles, SIDES, half_units, PACK, LANES), bf16),
            pltpu.VMEM((SIDES, half_units, PACK, LANES), bf16),
            pltpu.VMEM((half_units, PACK, LANES), bf16),
            pltpu.VMEM((levels, piece, PACK, LANES), bf16),
            pltpu.VMEM((levels - 1, piece, PACK, LANES), bf16),
            pltpu.VMEM((levels - 1, piece, PACK, LANES), bf16),
            pltpu.VMEM((tiles, SIDES, half_units, PACK, LANES), bf16),
            pltpu.VMEM((tiles, kept + 1, chips_az, cols, LANES), f32),
            pltpu.VMEM((2, units, PACK, LANES), bf16),
            pltpu.VMEM((2, units, PACK, LANES), bf16),
            pltpu.VMEM((2, kept * tiles * looks_rg, chips_az * LANES), f32),
            pltpu.VMEM(((kept + 1) * tiles * looks_rg, chips_az * LANES), f32),
            pltpu.VMEM((2, chips_az * LANES, LANES), bf16),
            pltpu.VMEM((n, share, LANES), f32),
            pltpu.VMEM((n, share, LANES), f32),
            pltpu.VMEM((share, n * kept + GROUP, LANES), f32),
            pltpu.VMEM((kinds, chips_rg, group_rows * GROUP, LANES), f32),
            dma((4,)), dma((3,)), dma((2, 4)), dma((2, 4)), dma((4,)), dma((4,)),
            dma((2, levels)), dma((2, levels)), dma((2, levels - 1)), dma((2, levels - 1)),
            dma((2,)), dma((2,)), dma((n,)), dma((n,)),
        ],
        compiler_params=pltpu.CompilerParams(
            collective_id=0, has_side_effects=True, vmem_limit_bytes=50 * 1024 * 1024
        ),
    )(frames, shifts.transpose(order), fractions.transpose(order), ref_dates[None])
    return (corr.transpose(order), coh.transpose(0, 4, 1, 2, 3))


def solution(mesh):
    return jax.shard_map(
        functools.partial(per_device, mesh.shape["date"], mesh.shape["strip"]),
        mesh=mesh,
        in_specs=(
            P("date", None, None, None, "strip"),
            P(None, "date", None, None, "strip"),
            P(None, "date", None, None, "strip"),
            P(),
        ),
        out_specs=(P(None, "date", None, None, "strip"), P(None, None, None, "date", "strip")),
        check_vma=False,
    )
```

time: 59.5 us -> 41.7 us (0.70)
  Pallas kernels: 52 us -> 35.4 us
  local copies, waits for them, and re-layouts: 6.42 us -> 4.91 us
    pallas_call x1, Pallas kernels: 52 us -> 35.4 us  [per_device(): pl.pallas_call(functools.partial(kernel, n, strips, (tiles, kept, chips_a...]
    unnamed x7 -> x10, local copies, waits for them, and re-layouts: 5.87 us -> 4.91 us
where the time goes in v1:
time: 41.7 us; the launch traced here: 41 us
  Pallas kernels  35.4 us (85%)
  local copies, waits for them, and re-layouts  4.91 us (12%)
  between operations  0.65 us (2%)
    pallas_call x1, Pallas kernels, per_device(): pl.pallas_call(functools.partial(kernel, n, strips, (tiles, kept, chips_a...  35.4 us
    unnamed x10, local copies, waits for them, and re-layouts  4.91 us

profile of v1, /device:TPU:0, one launch (start us, length us, event | category | flops | bytes accessed | tf_op | source)
XLA Modules:
  0.0 41.0 jit_solution(8208548285369988767)
XLA Ops:
  0.6 0.0 copy-start
  0.6 1.5 %copy-done = bf16[2,2,2,344,320]{3,4,2,1,0:T(8,128)(2,1)S(1)} copy-done((bf16[2,2,2,344,320]{3,4,2,1,0:T(8,128)(2,1)S(1)}, bf16[2,2,2,344,320]{3,4,2,1,0:T(8,128)(2,1)}, u32[]{:S(2)}) %copy-start) | copy-done | bytes 1761304
  2.2 0.0 copy-start.1
  2.2 0.7 %copy-done.1 = s32[2,2,2,5,5]{4,2,3,1,0:T(2,128)S(1)} copy-done((s32[2,2,2,5,5]{4,2,3,1,0:T(2,128)S(1)}, s32[2,2,2,5,5]{4,2,3,1,0:T(2,128)}, u32[]{:S(2)}) %copy-start.1) | copy-done | bytes 824
  2.9 0.0 copy-start.2
  2.9 0.7 %copy-done.2 = s32[2,2,2,5,5]{4,2,3,1,0:T(2,128)S(1)} copy-done((s32[2,2,2,5,5]{4,2,3,1,0:T(2,128)S(1)}, s32[2,2,2,5,5]{4,2,3,1,0:T(2,128)}, u32[]{:S(2)}) %copy-start.2) | copy-done | bytes 824
  3.6 0.0 copy-start.3
  3.6 0.7 %copy-done.3 = s32[2]{0:T(128)S(1)} copy-done((s32[2]{0:T(128)S(1)}, s32[2]{0:T(128)}, u32[]{:S(2)}) %copy-start.3) | copy-done | bytes 32
  4.3 35.4 %shard_map.59 = (f32[2,2,4,16,31]{4,3,2,1,0:T(8,128)S(1)}, f32[2,2,5,2,5]{4,3,2,1,0:T(2,128)S(1)}) custom-call(bf16[2,2,2,320,344]{4,3,2,1,0:T(8,128)(2,1)S(1)} %bitcast.6, s32[2,2,5,2,5]{4,3,2,1,0:T(2,128)S(1)} %bitcast.8, s32[2,2,5,2,5]{4,3,2,1,0:T(2,128)S(1)} %bitcast.9, s32[1,2]{1,0:T(1,128)S(1)} %bitcast.11), custom_call_target="tpu_custom_call" | custom-call | tf_op jit(solution)/shard_map/pallas_call | solution.py:635
  39.7 0.6 %copy.8 = f32[2,2,2,5,5]{4,2,3,1,0:T(2,128)} copy(f32[2,2,2,5,5]{4,2,3,1,0:T(2,128)S(1)} %bitcast.10) | data formatting | bytes 1600
  40.3 0.7 %copy.9 = f32[2,31,2,4,16]{1,4,3,2,0:T(8,128)} copy(f32[2,31,2,4,16]{1,4,3,2,0:T(8,128)S(1)} %bitcast.7) | data formatting | bytes 63488
Async XLA Ops:
  0.6 1.5 %copy-start = (bf16[2,2,2,344,320]{3,4,2,1,0:T(8,128)(2,1)S(1)}, bf16[2,2,2,344,320]{3,4,2,1,0:T(8,128)(2,1)}, u32[]{:S(2)}) copy-start(bf16[2,2,2,344,320]{3,4,2,1,0:T(8,128)(2,1)} %param.4) | copy-start | bytes 5283844
  2.2 0.7 %copy-start.1 = (s32[2,2,2,5,5]{4,2,3,1,0:T(2,128)S(1)}, s32[2,2,2,5,5]{4,2,3,1,0:T(2,128)}, u32[]{:S(2)}) copy-start(s32[2,2,2,5,5]{4,2,3,1,0:T(2,128)} %param.5) | copy-start | bytes 2404
  2.9 0.7 %copy-start.2 = (s32[2,2,2,5,5]{4,2,3,1,0:T(2,128)S(1)}, s32[2,2,2,5,5]{4,2,3,1,0:T(2,128)}, u32[]{:S(2)}) copy-start(s32[2,2,2,5,5]{4,2,3,1,0:T(2,128)} %param.6) | copy-start | bytes 2404
  3.6 0.7 %copy-start.3 = (s32[2]{0:T(128)S(1)}, s32[2]{0:T(128)}, u32[]{:S(2)}) copy-start(s32[2]{0:T(128)} %param.7) | copy-start | bytes 28

commit v2 on v1

--- a/solution.py
+++ b/solution.py
@@ -23,16 +23,29 @@
 SIDES = 2
 
 epsilon = 1e-06
+COS_TERMS = (1.0, -1 / 2, 1 / 24, -1 / 720, 1 / 40320, -1 / 3628800, 1 / 479001600, -1 / 87178291200)
 MESH = pl.DeviceIdType.MESH
 
 
+def half_turn_cos(square):
+    total = jnp.full(square.shape, COS_TERMS[-1], jnp.float32)
+    for term in COS_TERMS[-2::-1]:
+        total = total * square + term
+    return total
+
+
 def tap_weights(k, fraction):
-    distance = k.astype(jnp.float32) - (TAP_COUNT // 2 - 1) - fraction.astype(jnp.float32) / SUBSTEPS
+    part = fraction.astype(jnp.float32) / SUBSTEPS
+    distance = k.astype(jnp.float32) - (TAP_COUNT // 2 - 1) - part
+    turn = (part - 0.5) * jnp.pi
+    sine = half_turn_cos(turn * turn)
+    sine = jnp.where((k & 1) == 0, sine, -sine)
+    sine = jnp.where(part == 0.0, 0.0, sine)
     angle = jnp.pi * distance
-    sinc = jnp.where(
-        distance == 0.0, 1.0, jnp.sin(angle) / jnp.where(distance == 0.0, 1.0, angle)
-    )
-    weights = sinc * (0.5 + 0.5 * jnp.cos(jnp.pi * distance / (TAP_COUNT // 2)))
+    sinc = jnp.where(distance == 0.0, 1.0, sine / jnp.where(distance == 0.0, 1.0, angle))
+    eighth = distance * (jnp.pi / TAP_COUNT)
+    window = half_turn_cos(eighth * eighth)
+    weights = sinc * (window * window)
     weights = jnp.where((k >= 0) & (k < TAP_COUNT), weights, 0.0)
     return weights / jnp.sum(weights, axis=1, keepdims=True)
 
@@ -135,8 +148,105 @@
     def wide(count):
         return lax.broadcasted_iota(jnp.int32, (count, LANES), 1)
 
-    for copy in smalls:
-        copy.wait()
+    for y in range(SIDES):
+        used = (min(chips, (y + 1) * half_chips) - y * half_chips) * chip_units
+        if used < half_units:
+            for t in range(tiles):
+                cand[t, y, used:half_units] = jnp.zeros((half_units - used, PACK, LANES), bf16)
+
+
+    def move(depth, start, c):
+        source = lax.broadcasted_iota(jnp.int32, (depth, LANES), 0)
+        target = lax.broadcasted_iota(jnp.int32, (depth, LANES), 1)
+        mine = (target < CHIP_SIZE) if c == 0 else (target >= CHIP_SIZE)
+        hit = mine & (source == target - c * CHIP_SIZE + start)
+        return jnp.where(hit, 1.0, 0.0).astype(bf16)
+
+    def pick(t):
+        dates_row = dates_ref[0:1, :]
+        date_lane = lax.broadcasted_iota(jnp.int32, (1, tiles), 1)
+        date = jnp.sum(jnp.where(date_lane == t, dates_row, 0), axis=1, keepdims=True)
+        gains = [
+            jnp.broadcast_to(jnp.where(date == me * kept + d, 1.0, 0.0), (cols, frame.shape[4]))
+            .astype(bf16)
+            for d in range(kept)
+        ]
+        even = [move(LANES, MARGIN, c) for c in range(2)]
+        odd = [move(BAND, MARGIN + CHIP_SIZE, c) for c in range(2)]
+
+        parts = []
+        for c in range(2):
+            total = frame[0, t, c, inner, :] * gains[0]
+            for d in range(1, kept):
+                total = total + frame[d, t, c, inner, :] * gains[d]
+            parts.append(total)
+        for a in range(chips_az):
+            start = (a // 2) * LANES
+            depth = min(BAND if a % 2 else LANES, frame.shape[4] - start)
+            mixed = sum(
+                jnp.dot(
+                    parts[c][:, start : start + depth],
+                    (odd if a % 2 else even)[c][:depth],
+                    preferred_element_type=f32,
+                )
+                for c in range(2)
+            ).astype(bf16)
+            for r in range(chips_rg):
+                chip = a * chips_rg + r
+                unit = (chip % half_chips) * chip_units
+                value = mixed[r * CHIP_SIZE : (r + 1) * CHIP_SIZE]
+                cand[t, chip // half_chips, unit : unit + chip_units] = value.reshape(
+                    chip_units, PACK, LANES
+                )
+
+    smalls[2].wait()
+    loads[0].wait()
+    loads[1].wait()
+    pick(1 - core)
+
+    beside = jnp.minimum(strip, 1) + jnp.minimum(strips - 1 - strip, 1)
+    pl.semaphore_wait(barrier, n - 1 + beside)
+
+    core_rs = [
+        remote(cand.at[1 - core, y], core_in.at[y], core_send.at[i], core_recv.at[i],
+               device(level, side, 1 - core))
+        for i, y in enumerate((1 - side, side))
+    ]
+    for copy in core_rs:
+        copy.start()
+
+    order = ((core, core), (1 - core, 1 - core), (core, 1 - core), (1 - core, core))
+    edges = []
+    for i, (d, t) in enumerate(order):
+        up = remote(
+            frame_hbm.at[d, t, :, pl.ds(cols - HALO, HALO), :], frame.at[d, t, :, pl.ds(0, HALO), :],
+            edge_send.at[0, i], edge_recv.at[0, i], {"strip": strip + 1},
+        )
+        down = remote(
+            frame_hbm.at[d, t, :, pl.ds(0, HALO), :], frame.at[d, t, :, pl.ds(HALO + cols, HALO), :],
+            edge_send.at[1, i], edge_recv.at[1, i], {"strip": strip - 1},
+        )
+        edges.append((up, down))
+
+        @pl.when(has_high)
+        def _():
+            up.start()
+
+        @pl.when(has_low)
+        def _():
+            down.start()
+
+    def edge_wait(i):
+        @pl.when(has_low)
+        def _():
+            edges[i][0].wait_recv()
+
+        @pl.when(has_high)
+        def _():
+            edges[i][1].wait_recv()
+
+    smalls[0].wait()
+    smalls[1].wait()
 
     for d in range(kept):
         for a in range(chips_az):
@@ -155,101 +265,6 @@
         line_base[r, 0:spot_rows, :] = tap_weights(line_tap, values[2])
         col_tap = at - (values[1] + (first_tap + HALO - MARGIN))
         col_base[r, 0:spot_rows, :] = tap_weights(col_tap, values[3])
-
-    for y in range(SIDES):
-        used = (min(chips, (y + 1) * half_chips) - y * half_chips) * chip_units
-        if used < half_units:
-            for t in range(tiles):
-                cand[t, y, used:half_units] = jnp.zeros((half_units - used, PACK, LANES), bf16)
-
-    dates_row = dates_ref[0:1, :]
-
-    def pick(t):
-        def body(r, carry):
-            at = wide(CHIP_SIZE)
-            low = at < CHIP_SIZE
-            inside = at >= MARGIN
-            date_lane = lax.broadcasted_iota(jnp.int32, (1, tiles), 1)
-            date = jnp.sum(jnp.where(date_lane == t, dates_row, 0), axis=1, keepdims=True)
-            here = pl.ds(pl.multiple_of(HALO + r * CHIP_SIZE, PACK), CHIP_SIZE)
-            parts = []
-            for c in range(2):
-                total = None
-                for d in range(kept):
-                    gain = jnp.where(date == me * kept + d, 1.0, 0.0).astype(f32)
-                    value = frame[d, t, c, here, :].astype(f32) * gain
-                    total = value if total is None else total + value
-                blocks = []
-                for b in range(-(-total.shape[1] // LANES)):
-                    block = total[:, b * LANES : min((b + 1) * LANES, total.shape[1])]
-                    if block.shape[1] < LANES:
-                        block = jnp.concatenate(
-                            [block, jnp.zeros((CHIP_SIZE, LANES - block.shape[1]), f32)], axis=1
-                        )
-                    blocks.append(block)
-                parts.append(blocks)
-            for a in range(chips_az):
-                b = a // 2
-                moves = (LANES - MARGIN, CHIP_SIZE - MARGIN)
-                pair = [p[b] for p in parts]
-                if a % 2:
-                    moves = moves[::-1]
-                    pair = [jnp.where(inside, p[b], p[b + 1]) for p in parts]
-                pair = [pltpu.roll(v, m, 1) for v, m in zip(pair, moves)]
-                mixed = jnp.where(low, pair[0], pair[1]).astype(bf16)
-                chip = a * chips_rg + r
-                unit = (chip % half_chips) * chip_units
-                cand[t, chip // half_chips, pl.ds(unit, chip_units)] = mixed.reshape(
-                    chip_units, PACK, LANES
-                )
-            return carry
-
-        lax.fori_loop(0, chips_rg, body, 0)
-
-    loads[0].wait()
-    loads[1].wait()
-    pick(1 - core)
-
-    beside = jnp.minimum(strip, 1) + jnp.minimum(strips - 1 - strip, 1)
-    pl.semaphore_wait(barrier, n - 1 + beside)
-
-    core_rs = [
-        remote(cand.at[1 - core, y], core_in.at[y], core_send.at[i], core_recv.at[i],
-               device(level, side, 1 - core))
-        for i, y in enumerate((1 - side, side))
-    ]
-    for copy in core_rs:
-        copy.start()
-
-    order = ((core, core), (1 - core, 1 - core), (core, 1 - core), (1 - core, core))
-    edges = []
-    for i, (d, t) in enumerate(order):
-        up = remote(
-            frame_hbm.at[d, t, :, pl.ds(cols - HALO, HALO), :], frame.at[d, t, :, pl.ds(0, HALO), :],
-            edge_send.at[0, i], edge_recv.at[0, i], {"strip": strip + 1},
-        )
-        down = remote(
-            frame_hbm.at[d, t, :, pl.ds(0, HALO), :], frame.at[d, t, :, pl.ds(HALO + cols, HALO), :],
-            edge_send.at[1, i], edge_recv.at[1, i], {"strip": strip - 1},
-        )
-        edges.append((up, down))
-
-        @pl.when(has_high)
-        def _():
-            up.start()
-
-        @pl.when(has_low)
-        def _():
-            down.start()
-
-    def edge_wait(i):
-        @pl.when(has_low)
-        def _():
-            edges[i][0].wait_recv()
-
-        @pl.when(has_high)
-        def _():
-            edges[i][1].wait_recv()
 
     loads[2].wait()
     loads[3].wait()
@@ -329,7 +344,7 @@
         return wide(count) < CHIP_SIZE
 
     def chip_column(d, t, r, slot):
-        row0 = pl.multiple_of(r * CHIP_SIZE, CHIP_SIZE)
+        row0 = r * CHIP_SIZE
         window = pl.ds(row0, WINDOW)
 
         def base(ref, a):
@@ -382,11 +397,8 @@
     def resample(i, first, last):
         d, t = order[i]
 
-        def body(j, carry):
-            chip_column(d, t, lax.rem(j + 1, chips_rg), i if i < 2 else None)
-            return carry
-
-        lax.fori_loop(first, last, body, 0)
+        for j in range(first, last):
+            chip_column(d, t, (j + 1) % chips_rg, i if i < 2 else None)
 
     inside_cols = chips_rg - 2
     peer = me + 2 * core - 1
@@ -396,9 +408,8 @@
         sent.at[1], got.at[1], next_send.at[1], next_recv.at[1], device(level, side, 1 - core)
     )
 
-    resample(0, 0, 1)
     ref_core()
-    resample(0, 1, inside_cols)
+    resample(0, 0, inside_cols)
     edge_wait(0)
     resample(0, inside_cols, chips_rg)
 
@@ -406,14 +417,15 @@
     def _():
         outward.start()
 
-    ref_side(0)
     resample(1, 0, inside_cols)
     edge_wait(1)
     resample(1, inside_cols, chips_rg)
     inward.start()
+    ref_side(0)
+    resample(2, 0, inside_cols)
     ref_side(1)
     edge_wait(2)
-    resample(2, 0, chips_rg)
+    resample(2, inside_cols, chips_rg)
     for k in range(2, len(steps)):
         ref_side(k)
     edge_wait(3)
@@ -426,7 +438,7 @@
         return series[t, pos, a, pl.ds(s, looks_rg, stride=LOOK_RG), :]
 
     def look(t, early, wanted):
-        def body(a, carry):
+        for a in range(chips_az):
             sums = [jnp.zeros((looks_rg, LANES), f32) for _ in range(2 + len(wanted))]
             for s in range(LOOK_RG):
                 first = pick_rows(t, early, a, s)
@@ -436,16 +448,13 @@
                 for i, pos in enumerate(wanted):
                     value = pick_rows(t, pos, a, s)
                     sums[2 + i] = sums[2 + i] + value * value
-            span = pl.ds(pl.multiple_of(a * LANES, LANES), LANES)
+            span = slice(a * LANES, (a + 1) * LANES)
             row = pl.multiple_of((early * tiles + t) * looks_rg, GROUP)
             for c in range(2):
                 cross_sums[c, pl.ds(row, looks_rg), span] = sums[c]
             for i, pos in enumerate(wanted):
                 row = pl.multiple_of((pos * tiles + t) * looks_rg, GROUP)
                 powers[pl.ds(row, looks_rg), span] = sums[2 + i]
-            return carry
-
-        lax.fori_loop(0, chips_az, body, 0)
 
     def unpack(i, t, pos):
         def body(j, carry):
@@ -475,10 +484,34 @@
 
     lax.fori_loop(0, chips_az, build_selectors, 0)
 
+    def correlate(t, y):
+        for j in reversed(range(half_chips)):
+            chip = jnp.minimum(y * half_chips + j, chips - 1)
+            a = chip // chips_rg
+            r = chip % chips_rg
+            row = pl.multiple_of(r * CHIP_SIZE, CHIP_SIZE)
+            to = pl.ds(pl.multiple_of((a * tiles + t) * GROUP, GROUP), GROUP)
+            sums = [None] * (1 + 2 * kept)
+            for g in range(chip_units):
+                ref = whole[t, y, j * chip_units + g].astype(f32)
+                turned = pltpu.roll(ref, CHIP_SIZE, 1)
+                terms = [ref * ref]
+                for d in range(kept):
+                    value = series[t, d + t, a, pl.ds(row + g * PACK, PACK), :]
+                    terms += [ref * value, turned * value]
+                for k, term in enumerate(terms):
+                    term = term[:GROUP] + term[GROUP:]
+                    sums[k] = term if sums[k] is None else sums[k] + term
+            for k, value in enumerate(sums):
+                totals[k, r, to, :] = value
+
     inward.wait_recv()
     unpack(1, core, 2 * (1 - core))
     look(core, 1 - core, (2 * (1 - core),))
     ref_level()
+    for k in range(len(steps)):
+        ref_back(k)
+    correlate(core, side)
 
     @pl.when(has_peer)
     def _():
@@ -510,34 +543,6 @@
         copy.start()
         relays.append(copy)
 
-    for k in range(len(steps)):
-        ref_back(k)
-
-    def correlate(t, y):
-        def body(j, carry):
-            chip = y * half_chips + j
-            a = chip // chips_rg
-            r = chip % chips_rg
-            ref = whole[t, y, pl.ds(j * chip_units, chip_units)]
-            ref = ref.reshape(CHIP_SIZE, LANES).astype(f32)
-            turned = pltpu.roll(ref, CHIP_SIZE, 1)
-            row = pl.multiple_of(r * CHIP_SIZE, CHIP_SIZE)
-            to = pl.ds(pl.multiple_of((a * tiles + t) * GROUP, GROUP), GROUP)
-
-            def put(k, value):
-                total = jnp.sum(value.reshape(GROUP, GROUP, LANES), axis=0)
-                totals[k, r, to, :] = total
-
-            put(0, ref * ref)
-            for d in range(kept):
-                value = series[t, d + t, a, pl.ds(row, CHIP_SIZE), :]
-                put(1 + 2 * d, ref * value)
-                put(2 + 2 * d, turned * value)
-            return carry
-
-        lax.fori_loop(0, jnp.minimum(half_chips, chips - y * half_chips), body, 0)
-
-    correlate(core, side)
     ref_other()
     correlate(core, 1 - side)
     core_ag[0].wait_recv()
@@ -638,7 +643,7 @@
             jax.ShapeDtypeStruct((2, tiles, share, looks_rg, n * kept - 1), f32),
             jax.ShapeDtypeStruct((2, kept, chips_az, tiles, chips_rg), f32),
         ),
-        in_specs=[pl.BlockSpec(memory_space=pl.ANY)] * 4,
+        in_specs=[pl.BlockSpec(memory_space=pltpu.HBM)] * 4,
         out_specs=(vmem, vmem),
         scratch_shapes=[
             pltpu.VMEM((kept, tiles, 2, cols + 2 * HALO, all_rows), bf16),
@@ -672,7 +677,7 @@
         compiler_params=pltpu.CompilerParams(
             collective_id=0, has_side_effects=True, vmem_limit_bytes=50 * 1024 * 1024
         ),
-    )(frames, shifts.transpose(order), fractions.transpose(order), ref_dates[None])
+    )(*[pltpu.with_memory_space_constraint(v, pltpu.HBM) for v in (frames, shifts.transpose(order), fractions.transpose(order), ref_dates[None])])
     return (corr.transpose(order), coh.transpose(0, 4, 1, 2, 3))
 
 

time: 41.7 us -> 35 us (0.84); the launches traced: 41 us -> 34.8 us
  local copies, waits for them, and re-layouts: 4.91 us -> 1.26 us
  Pallas kernels: 35.4 us -> 32.9 us
    unnamed x10 -> x2, local copies, waits for them, and re-layouts: 4.91 us -> 1.26 us
    pallas_call x1, Pallas kernels: 35.4 us -> 32.9 us  [per_device(): pl.pallas_call(functools.partial(kernel, n, strips, (tiles, kept, chips_a...]
where the time goes in v2:
time: 35 us; the launch traced here: 34.8 us
  Pallas kernels  32.9 us (94%)
  local copies, waits for them, and re-layouts  1.26 us (4%)
  between operations  0.64 us (2%)
    pallas_call x1, Pallas kernels, per_device(): pl.pallas_call(functools.partial(kernel, n, strips, (tiles, kept, chips_a...  32.9 us
    unnamed x2, local copies, waits for them, and re-layouts  1.26 us

profile of v2, /device:TPU:0, one launch (start us, length us, event | category | flops | bytes accessed | tf_op | source)
XLA Modules:
  0.0 34.8 jit_solution(1599352987252422526)
XLA Ops:
  0.6 32.9 %shard_map.59 = (f32[2,2,4,16,31]{4,3,2,1,0:T(8,128)S(1)}, f32[2,2,5,2,5]{4,3,2,1,0:T(2,128)S(1)}) custom-call(bf16[2,2,2,320,344]{4,3,2,1,0:T(8,128)(2,1)} %bitcast.8, s32[2,2,5,2,5]{4,3,2,1,0:T(2,128)} %bitcast.9, s32[2,2,5,2,5]{4,3,2,1,0:T(2,128)} %bitcast.10, s32[1,2]{1,0:T(1,128)} %bitcast.11), custom_call_target="tpu_custom_call" | custom-call | tf_op jit(solution)/shard_map/pallas_call | solution.py:640
  33.5 0.6 %copy.8 = f32[2,2,2,5,5]{4,2,3,1,0:T(2,128)} copy(f32[2,2,2,5,5]{4,2,3,1,0:T(2,128)S(1)} %bitcast.7) | data formatting | bytes 1600
  34.2 0.7 %copy.9 = f32[2,31,2,4,16]{1,4,3,2,0:T(8,128)} copy(f32[2,31,2,4,16]{1,4,3,2,0:T(8,128)S(1)} %bitcast.6) | data formatting | bytes 63488

commit v3 on v2

--- a/solution.py
+++ b/solution.py
@@ -21,6 +21,8 @@
 BAND = 160
 CORES = 2
 SIDES = 2
+EARLY = 2
+SHARE = 36
 
 epsilon = 1e-06
 COS_TERMS = (1.0, -1 / 2, 1 / 24, -1 / 720, 1 / 40320, -1 / 3628800, 1 / 479001600, -1 / 87178291200)
@@ -68,10 +70,10 @@
     frame_hbm, shifts_hbm, fractions_hbm, dates_hbm,
     coh_ref, corr_ref,
     frame, shifts_ref, fractions_ref, dates_ref, spots, line_base, col_base,
-    cand, core_in, y_out, y_in, z_out, z_in, whole,
+    cand, core_in, y_out, y_in, z_out, z_in, across_out, across_in, over, over_in, whole,
     series, sent, got, cross_sums, powers, selectors, out_buf, coh_in, ordered, totals,
     load_sem, small_sem, edge_send, edge_recv, core_send, core_recv, y_send, y_recv,
-    z_send, z_recv, next_send, next_recv, coh_send, coh_recv,
+    z_send, z_recv, side_recv, back_recv, next_send, next_recv, coh_send, coh_recv,
 ):
     tiles, kept, chips_az, chips_rg, rows, cols = dims
     me = lax.axis_index("date")
@@ -84,9 +86,11 @@
     f32 = jnp.float32
     chips = chips_az * chips_rg
     chip_units = CHIP_SIZE // PACK
-    half_chips = -(-chips // SIDES)
-    half_units = whole.shape[2]
-    piece = half_units // levels
+    piece, strip_piece = y_in.shape[1], across_in.shape[1]
+    half_units = levels * piece
+    half_chips = half_units // chip_units
+    tail_first = SIDES * half_chips
+    tail = pl.ds(SIDES * half_units, levels * strip_piece)
     steps = [levels // 2] + [o for o in range(1, levels) if o != levels // 2]
 
     def at_level(o):
@@ -102,26 +106,35 @@
         )
 
     inner = pl.ds(HALO, cols)
-    loads = {}
-    for i, (d, t) in enumerate(((core, 1 - core), (1 - core, 1 - core), (core, core), (1 - core, core))):
-        loads[i] = pltpu.make_async_copy(
-            frame_hbm.at[d, t], frame.at[d, t, :, inner, :], load_sem.at[i]
+    dates_copy = pltpu.make_async_copy(dates_hbm, dates_ref, small_sem.at[0])
+    dates_copy.start()
+    loads = []
+    for i, t in enumerate((1 - core, core)):
+        loads.append(
+            pltpu.make_async_copy(
+                frame_hbm.at[:, t], frame.at[:, t, :, inner, :], load_sem.at[i]
+            )
         )
         loads[i].start()
     smalls = [
-        pltpu.make_async_copy(src, dst, small_sem.at[i])
-        for i, (src, dst) in enumerate(
-            ((shifts_hbm, shifts_ref), (fractions_hbm, fractions_ref), (dates_hbm, dates_ref))
-        )
+        pltpu.make_async_copy(shifts_hbm, shifts_ref, small_sem.at[1]),
+        pltpu.make_async_copy(fractions_hbm, fractions_ref, small_sem.at[2]),
     ]
     for copy in smalls:
         copy.start()
 
     barrier = pltpu.get_barrier_semaphore()
-    for o in range(1, n):
-        pl.semaphore_signal(
-            barrier, inc=1, device_id={"date": lax.rem(me + o, n)}, device_id_type=MESH
-        )
+    peer = me + 2 * core - 1
+    has_peer = (peer >= 0) & (peer < n)
+    near = [device(level, side, 1 - core), device(level, 1 - side, core)]
+    near += [device(at_level(o), side, core) for o in range(1, levels)]
+    for where in near:
+        pl.semaphore_signal(barrier, inc=1, device_id=where, device_id_type=MESH)
+
+    @pl.when(has_peer)
+    def _():
+        pl.semaphore_signal(barrier, inc=1, device_id={"date": peer}, device_id_type=MESH)
+
     has_low = strip > 0
     has_high = strip < strips - 1
 
@@ -148,12 +161,14 @@
     def wide(count):
         return lax.broadcasted_iota(jnp.int32, (count, LANES), 1)
 
-    for y in range(SIDES):
-        used = (min(chips, (y + 1) * half_chips) - y * half_chips) * chip_units
-        if used < half_units:
-            for t in range(tiles):
-                cand[t, y, used:half_units] = jnp.zeros((half_units - used, PACK, LANES), bf16)
-
+    def half(y):
+        return pl.ds(y * half_units, half_units)
+
+    used = chips * chip_units
+    spare = cand.shape[1] - used
+    if spare:
+        for t in range(tiles):
+            cand[t, used:] = jnp.zeros((spare, PACK, LANES), bf16)
 
     def move(depth, start, c):
         source = lax.broadcasted_iota(jnp.int32, (depth, LANES), 0)
@@ -161,6 +176,9 @@
         mine = (target < CHIP_SIZE) if c == 0 else (target >= CHIP_SIZE)
         hit = mine & (source == target - c * CHIP_SIZE + start)
         return jnp.where(hit, 1.0, 0.0).astype(bf16)
+
+    even = [move(LANES, MARGIN, c) for c in range(2)]
+    odd = [move(BAND, MARGIN + CHIP_SIZE, c) for c in range(2)]
 
     def pick(t):
         dates_row = dates_ref[0:1, :]
@@ -171,9 +189,6 @@
             .astype(bf16)
             for d in range(kept)
         ]
-        even = [move(LANES, MARGIN, c) for c in range(2)]
-        odd = [move(BAND, MARGIN + CHIP_SIZE, c) for c in range(2)]
-
         parts = []
         for c in range(2):
             total = frame[0, t, c, inner, :] * gains[0]
@@ -192,25 +207,23 @@
                 for c in range(2)
             ).astype(bf16)
             for r in range(chips_rg):
-                chip = a * chips_rg + r
-                unit = (chip % half_chips) * chip_units
-                value = mixed[r * CHIP_SIZE : (r + 1) * CHIP_SIZE]
-                cand[t, chip // half_chips, unit : unit + chip_units] = value.reshape(
-                    chip_units, PACK, LANES
-                )
-
-    smalls[2].wait()
+                unit = (r * chips_az + a) * chip_units
+                cand[t, unit : unit + chip_units] = mixed[
+                    r * CHIP_SIZE : (r + 1) * CHIP_SIZE
+                ].reshape(chip_units, PACK, LANES)
+
+    dates_copy.wait()
     loads[0].wait()
-    loads[1].wait()
     pick(1 - core)
 
     beside = jnp.minimum(strip, 1) + jnp.minimum(strips - 1 - strip, 1)
-    pl.semaphore_wait(barrier, n - 1 + beside)
+    linked = jnp.where(has_peer, 1, 0)
+    pl.semaphore_wait(barrier, len(near) + linked + beside)
 
     core_rs = [
-        remote(cand.at[1 - core, y], core_in.at[y], core_send.at[i], core_recv.at[i],
+        remote(cand.at[1 - core, span], core_in.at[span], core_send.at[0], core_recv.at[i],
                device(level, side, 1 - core))
-        for i, y in enumerate((1 - side, side))
+        for i, span in enumerate((half(1 - side), tail, half(side)))
     ]
     for copy in core_rs:
         copy.start()
@@ -220,11 +233,11 @@
     for i, (d, t) in enumerate(order):
         up = remote(
             frame_hbm.at[d, t, :, pl.ds(cols - HALO, HALO), :], frame.at[d, t, :, pl.ds(0, HALO), :],
-            edge_send.at[0, i], edge_recv.at[0, i], {"strip": strip + 1},
+            edge_send.at[0], edge_recv.at[0, i], {"strip": strip + 1},
         )
         down = remote(
             frame_hbm.at[d, t, :, pl.ds(0, HALO), :], frame.at[d, t, :, pl.ds(HALO + cols, HALO), :],
-            edge_send.at[1, i], edge_recv.at[1, i], {"strip": strip - 1},
+            edge_send.at[1], edge_recv.at[1, i], {"strip": strip - 1},
         )
         edges.append((up, down))
 
@@ -244,6 +257,121 @@
         @pl.when(has_high)
         def _():
             edges[i][1].wait_recv()
+
+    loads[1].wait()
+    pick(core)
+
+    def level_piece(y, z):
+        return pl.ds(y * half_units + z * piece, piece)
+
+    y_rs = [
+        remote(y_out.at[level_piece(0, at_level(o))], y_in.at[k], y_send.at[0], side_recv.at[k],
+               device(level, 1 - side, core))
+        for k, o in enumerate(steps + [0])
+    ]
+    z_rs = [
+        remote(z_out.at[k], z_in.at[k], z_send.at[0], z_recv.at[0],
+               device(at_level(o), side, core))
+        for k, o in enumerate(steps)
+    ]
+    mine = whole.at[core, level_piece(side, level)]
+    z_ag = [
+        remote(mine, mine, z_send.at[1], back_recv.at[k], device(at_level(o), side, core))
+        for k, o in enumerate(steps)
+    ]
+    y_ag = []
+    for k, o in enumerate(steps + [0]):
+        part = whole.at[core, level_piece(side, at_level(levels - o))]
+        y_ag.append(
+            remote(part, part, y_send.at[1], y_recv.at[1], device(level, 1 - side, core))
+        )
+    core_ag = [
+        remote(whole.at[core, span], whole.at[core, span], core_send.at[1], core_recv.at[3 + i],
+               device(level, side, 1 - core))
+        for i, span in enumerate((half(side), half(1 - side), tail))
+    ]
+
+    def tail_piece(z):
+        return pl.ds(SIDES * half_units + z * strip_piece, strip_piece)
+
+    tail_rs = [
+        remote(across_out.at[pl.ds(at_level(o) * strip_piece, strip_piece)], across_in.at[k],
+               z_send.at[2], z_recv.at[2], device(at_level(o), side, core))
+        for k, o in enumerate(steps)
+    ]
+    tail_y = remote(over, over_in, y_send.at[2], y_recv.at[2], device(level, 1 - side, core))
+    tail_mine = whole.at[core, tail_piece(level)]
+    tail_ag = [
+        remote(tail_mine, tail_mine, z_send.at[3], z_recv.at[3], device(at_level(o), side, core))
+        for o in steps
+    ]
+
+    def all_of(ref, send, recv):
+        return remote(ref, ref, send, recv, device(level, side, core))
+
+    def tail_core():
+        core_rs[1].wait_recv()
+        across_out[...] = cand[core, tail] + core_in[tail]
+        for copy in tail_rs:
+            copy.start()
+
+    def tail_side():
+        all_of(across_in, z_send.at[2], z_recv.at[2]).wait_recv()
+        total = across_out[pl.ds(level * strip_piece, strip_piece)]
+        for k in range(len(steps)):
+            total = total + across_in[k]
+        over[...] = total
+        tail_y.start()
+
+    def tail_level():
+        tail_y.wait_recv()
+        whole[core, tail_piece(level)] = over[...] + over_in[...]
+        for copy in tail_ag:
+            copy.start()
+
+    def tail_back():
+        all_of(across_in, z_send.at[3], z_recv.at[3]).wait_recv()
+        core_ag[2].start()
+
+    def ref_core():
+        core_rs[0].wait_recv()
+        y_out[...] = cand[core, half(1 - side)] + core_in[half(1 - side)]
+        for copy in y_rs:
+            copy.start()
+
+    def piece_sum(k, o):
+        at = level_piece(side, at_level(o))
+        y_rs[k].wait_recv()
+        return cand[core, at] + core_in[at] + y_in[k]
+
+    def ref_side(k):
+        if k == 0:
+            core_rs[2].wait_recv()
+        z_out[k] = piece_sum(k, steps[k])
+        z_rs[k].start()
+
+    def ref_level():
+        total = piece_sum(len(steps), 0)
+        all_of(z_in, z_send.at[0], z_recv.at[0]).wait_recv()
+        for k in range(len(steps)):
+            total = total + z_in[k]
+        whole[core, level_piece(side, level)] = total
+        for copy in z_ag:
+            copy.start()
+        y_ag[len(steps)].start()
+
+    def ref_back(k):
+        z_ag[k].wait_recv()
+        y_ag[k].start()
+        if k == len(steps) - 1:
+            core_ag[0].start()
+
+    def ref_other():
+        all_of(y_out, y_send.at[1], y_recv.at[1]).wait_recv()
+        core_ag[1].start()
+
+    ref_core()
+    tail_core()
 
     smalls[0].wait()
     smalls[1].wait()
@@ -265,78 +393,6 @@
         line_base[r, 0:spot_rows, :] = tap_weights(line_tap, values[2])
         col_tap = at - (values[1] + (first_tap + HALO - MARGIN))
         col_base[r, 0:spot_rows, :] = tap_weights(col_tap, values[3])
-
-    loads[2].wait()
-    loads[3].wait()
-    pick(core)
-
-    def level_piece(z):
-        return pl.ds(z * piece, piece)
-
-    y_rs = [
-        remote(y_out.at[level_piece(at_level(o))], y_in.at[k], y_send.at[0, k], y_recv.at[0, k],
-               device(level, 1 - side, core))
-        for k, o in enumerate(steps + [0])
-    ]
-    z_rs = [
-        remote(z_out.at[k], z_in.at[k], z_send.at[0, k], z_recv.at[0, k],
-               device(at_level(o), side, core))
-        for k, o in enumerate(steps)
-    ]
-    mine = whole.at[core, side, level_piece(level)]
-    z_ag = [
-        remote(mine, mine, z_send.at[1, k], z_recv.at[1, k], device(at_level(o), side, core))
-        for k, o in enumerate(steps)
-    ]
-    y_ag = []
-    for k, o in enumerate(steps + [0]):
-        part = whole.at[core, side, level_piece(at_level(levels - o))]
-        y_ag.append(
-            remote(part, part, y_send.at[1, k], y_recv.at[1, k], device(level, 1 - side, core))
-        )
-    core_ag = [
-        remote(whole.at[core, y], whole.at[core, y], core_send.at[2 + i], core_recv.at[2 + i],
-               device(level, side, 1 - core))
-        for i, y in enumerate((side, 1 - side))
-    ]
-
-    def ref_core():
-        core_rs[0].wait_recv()
-        y_out[...] = cand[core, 1 - side] + core_in[1 - side]
-        for copy in y_rs:
-            copy.start()
-
-    def piece_sum(k, o):
-        at = level_piece(at_level(o))
-        y_rs[k].wait_recv()
-        return cand[core, side, at] + core_in[side, at] + y_in[k]
-
-    def ref_side(k):
-        if k == 0:
-            core_rs[1].wait_recv()
-        z_out[k] = piece_sum(k, steps[k])
-        z_rs[k].start()
-
-    def ref_level():
-        total = piece_sum(len(steps), 0)
-        for k in range(len(steps)):
-            z_rs[k].wait_recv()
-            total = total + z_in[k]
-        whole[core, side, level_piece(level)] = total
-        for copy in z_ag:
-            copy.start()
-        y_ag[len(steps)].start()
-
-    def ref_back(k):
-        z_ag[k].wait_recv()
-        y_ag[k].start()
-        if k == len(steps) - 1:
-            core_ag[0].start()
-
-    def ref_other():
-        for copy in y_ag:
-            copy.wait_recv()
-        core_ag[1].start()
 
     low_lane = wide(CHIP_SIZE) < CHIP_SIZE
 
@@ -387,7 +443,7 @@
             matrix = spread(base(col_base, a), CHIP_SIZE, 0)[:, :WINDOW].astype(bf16)
             out = jnp.dot(matrix, partial[a], preferred_element_type=f32).astype(bf16)
             if slot is not None:
-                unit = (a * chips_rg + r) * chip_units
+                unit = (r * chips_az + a) * chip_units
                 sent[slot, pl.ds(unit, chip_units)] = out.reshape(chip_units, PACK, LANES)
             out = out.astype(f32)
             series[t, d + t, a, pl.ds(row0, CHIP_SIZE), :] = out
@@ -401,33 +457,44 @@
             chip_column(d, t, (j + 1) % chips_rg, i if i < 2 else None)
 
     inside_cols = chips_rg - 2
-    peer = me + 2 * core - 1
-    has_peer = (peer >= 0) & (peer < n)
-    outward = remote(sent.at[0], got.at[0], next_send.at[0], next_recv.at[0], {"date": peer})
+    column = chips_az * chip_units
+    outward = []
+    for r in range(chips_rg):
+        span = pl.ds(r * column, column)
+        outward.append(
+            remote(sent.at[0, span], got.at[0, span], next_send.at[0], next_recv.at[0], {"date": peer})
+        )
+
+    def outward_start(first, last):
+        @pl.when(has_peer)
+        def _():
+            for r in range(first, last):
+                outward[r].start()
+
+    def outward_all():
+        return remote(sent.at[0], got.at[0], next_send.at[0], next_recv.at[0], {"date": peer})
+
     inward = remote(
         sent.at[1], got.at[1], next_send.at[1], next_recv.at[1], device(level, side, 1 - core)
     )
 
-    ref_core()
     resample(0, 0, inside_cols)
+    ref_side(0)
     edge_wait(0)
     resample(0, inside_cols, chips_rg)
-
-    @pl.when(has_peer)
-    def _():
-        outward.start()
-
+    ref_side(1)
     resample(1, 0, inside_cols)
+    for k in range(2, len(steps)):
+        ref_side(k)
+    outward_start(0, EARLY)
     edge_wait(1)
     resample(1, inside_cols, chips_rg)
     inward.start()
-    ref_side(0)
+    tail_side()
+    outward_start(EARLY, chips_rg)
     resample(2, 0, inside_cols)
-    ref_side(1)
     edge_wait(2)
     resample(2, inside_cols, chips_rg)
-    for k in range(2, len(steps)):
-        ref_side(k)
     edge_wait(3)
     resample(3, 0, chips_rg)
 
@@ -459,7 +526,7 @@
     def unpack(i, t, pos):
         def body(j, carry):
             for a in range(chips_az):
-                unit = a * chips_rg * chip_units + j * chip_units
+                unit = (j * chips_az + a) * chip_units
                 value = got[i, pl.ds(unit, chip_units)].reshape(CHIP_SIZE, LANES)
                 row = pl.multiple_of(j * CHIP_SIZE, CHIP_SIZE)
                 series[t, pos, a, pl.ds(row, CHIP_SIZE), :] = value.astype(f32)
@@ -467,8 +534,7 @@
 
         lax.fori_loop(0, chips_rg, body, 0)
 
-    look(0, 0, (0, 1))
-    look(1, 1, (1, 2))
+    look(1 - core, 1 - core, (1 - core, 2 - core))
 
     def build_selectors(a, carry):
         line = lax.broadcasted_iota(jnp.int32, (LANES, LANES), 0)
@@ -484,16 +550,16 @@
 
     lax.fori_loop(0, chips_az, build_selectors, 0)
 
-    def correlate(t, y):
-        for j in reversed(range(half_chips)):
-            chip = jnp.minimum(y * half_chips + j, chips - 1)
-            a = chip // chips_rg
-            r = chip % chips_rg
+    def correlate(t, first, count):
+        for j in range(count):
+            chip = first + j
+            a = chip % chips_az
+            r = chip // chips_az
             row = pl.multiple_of(r * CHIP_SIZE, CHIP_SIZE)
             to = pl.ds(pl.multiple_of((a * tiles + t) * GROUP, GROUP), GROUP)
             sums = [None] * (1 + 2 * kept)
             for g in range(chip_units):
-                ref = whole[t, y, j * chip_units + g].astype(f32)
+                ref = whole[t, chip * chip_units + g].astype(f32)
                 turned = pltpu.roll(ref, CHIP_SIZE, 1)
                 terms = [ref * ref]
                 for d in range(kept):
@@ -505,17 +571,16 @@
             for k, value in enumerate(sums):
                 totals[k, r, to, :] = value
 
+    ref_level()
+    tail_level()
+    look(core, core, (core, 1 + core))
     inward.wait_recv()
     unpack(1, core, 2 * (1 - core))
     look(core, 1 - core, (2 * (1 - core),))
-    ref_level()
-    for k in range(len(steps)):
-        ref_back(k)
-    correlate(core, side)
 
     @pl.when(has_peer)
     def _():
-        outward.wait_recv()
+        outward_all().wait_recv()
         unpack(0, 1 - core, 2 * core)
 
     @pl.when(jnp.logical_not(has_peer))
@@ -534,21 +599,27 @@
     for j in range(n):
         out_buf[j] = coherence[j * share : (j + 1) * share]
     coh_in[me] = out_buf[me]
-    relays = []
     for o in range(1, n):
         to = lax.rem(me + o, n)
         copy = remote(
-            out_buf.at[to], coh_in.at[me], coh_send.at[o], coh_recv.at[o], {"date": to}
+            out_buf.at[to], coh_in.at[me], coh_send.at[0], coh_recv.at[0], {"date": to}
         )
         copy.start()
-        relays.append(copy)
-
+
+    for k in range(len(steps)):
+        ref_back(k)
+    tail_back()
+    tail_chips = chips - tail_first
+    correlate(core, side * half_chips, half_chips)
+    correlate(core, tail_first, tail_chips)
+    core_ag[0].wait_recv()
+    correlate(1 - core, side * half_chips, half_chips)
+    core_ag[2].wait_recv()
+    correlate(1 - core, tail_first, tail_chips)
     ref_other()
-    correlate(core, 1 - side)
-    core_ag[0].wait_recv()
-    correlate(1 - core, side)
+    correlate(core, (1 - side) * half_chips, half_chips)
     core_ag[1].wait_recv()
-    correlate(1 - core, 1 - side)
+    correlate(1 - core, (1 - side) * half_chips, half_chips)
 
     kinds = totals.shape[0]
     group_rows = totals.shape[2] // GROUP
@@ -581,8 +652,11 @@
             for a in range(chips_az):
                 corr_ref[c, d, a] = value[a * tiles : (a + 1) * tiles, :chips_rg]
 
-    for copy in relays:
-        copy.wait_recv()
+    others = pl.ds(0, n - 1)
+    relays = remote(
+        out_buf.at[others], coh_in.at[others], coh_send.at[0], coh_recv.at[0], {"date": me}
+    )
+    relays.wait_recv()
     pairs = n * kept
     lane_n = wide(n)
     for y in range(share):
@@ -598,21 +672,34 @@
                 row = c * kept * tiles * looks_rg + t * looks_rg
                 coh_ref[c, t, y] = value[row : row + looks_rg, : pairs - 1]
 
-    for copy in relays + core_rs + y_rs + z_rs + z_ag + y_ag + core_ag + [inward]:
-        copy.wait_send()
+    relays.wait_send()
+    inward.wait_send()
+    for ref, sem in (
+        (cand.at[1 - core], core_send.at[0]),
+        (whole.at[core], core_send.at[1]),
+        (y_out, y_send.at[0]),
+        (y_out, y_send.at[1]),
+        (over, y_send.at[2]),
+        (z_out, z_send.at[0]),
+        (z_out, z_send.at[1]),
+        (across_in, z_send.at[2]),
+        (across_in, z_send.at[3]),
+    ):
+        all_of(ref, sem, sem).wait_send()
 
     @pl.when(has_peer)
     def _():
-        outward.wait_send()
-
-    for up, down in edges:
-        @pl.when(has_high)
-        def _():
-            up.wait_send()
-
-        @pl.when(has_low)
-        def _():
-            down.wait_send()
+        outward_all().wait_send()
+
+    rim = frame.at[:, :, :, 0:HALO, :]
+
+    @pl.when(has_high)
+    def _():
+        all_of(rim, edge_send.at[0], edge_send.at[0]).wait_send()
+
+    @pl.when(has_low)
+    def _():
+        all_of(rim, edge_send.at[1], edge_send.at[1]).wait_send()
 
 
 def per_device(n, strips, acquisitions, shifts, fractions, ref_dates):
@@ -622,9 +709,10 @@
     chips = chips_az * chips_rg
     units = chips * CHIP_SIZE // PACK
     levels = n // (CORES * SIDES)
-    half_chips = -(-chips // SIDES)
-    piece = -(-(half_chips * CHIP_SIZE // PACK) // levels)
+    piece = max(units * SHARE // 100 // levels, 1)
     half_units = piece * levels
+    strip_piece = -(-(units - SIDES * half_units) // levels)
+    total_units = SIDES * half_units + levels * strip_piece
     looks_rg = cols // LOOK_RG
     look_rows = rows // LOOK_AZ
     share = look_rows // n
@@ -653,13 +741,17 @@
             pltpu.VMEM((4, spot_rows, LANES), jnp.int32),
             pltpu.VMEM((chips_rg, spot_rows, LANES), f32),
             pltpu.VMEM((chips_rg, spot_rows, LANES), f32),
-            pltpu.VMEM((tiles, SIDES, half_units, PACK, LANES), bf16),
-            pltpu.VMEM((SIDES, half_units, PACK, LANES), bf16),
+            pltpu.VMEM((tiles, total_units, PACK, LANES), bf16),
+            pltpu.VMEM((total_units, PACK, LANES), bf16),
             pltpu.VMEM((half_units, PACK, LANES), bf16),
             pltpu.VMEM((levels, piece, PACK, LANES), bf16),
             pltpu.VMEM((levels - 1, piece, PACK, LANES), bf16),
             pltpu.VMEM((levels - 1, piece, PACK, LANES), bf16),
-            pltpu.VMEM((tiles, SIDES, half_units, PACK, LANES), bf16),
+            pltpu.VMEM((levels * strip_piece, PACK, LANES), bf16),
+            pltpu.VMEM((levels - 1, strip_piece, PACK, LANES), bf16),
+            pltpu.VMEM((strip_piece, PACK, LANES), bf16),
+            pltpu.VMEM((strip_piece, PACK, LANES), bf16),
+            pltpu.VMEM((tiles, total_units, PACK, LANES), bf16),
             pltpu.VMEM((tiles, kept + 1, chips_az, cols, LANES), f32),
             pltpu.VMEM((2, units, PACK, LANES), bf16),
             pltpu.VMEM((2, units, PACK, LANES), bf16),
@@ -670,9 +762,9 @@
             pltpu.VMEM((n, share, LANES), f32),
             pltpu.VMEM((share, n * kept + GROUP, LANES), f32),
             pltpu.VMEM((kinds, chips_rg, group_rows * GROUP, LANES), f32),
-            dma((4,)), dma((3,)), dma((2, 4)), dma((2, 4)), dma((4,)), dma((4,)),
-            dma((2, levels)), dma((2, levels)), dma((2, levels - 1)), dma((2, levels - 1)),
-            dma((2,)), dma((2,)), dma((n,)), dma((n,)),
+            dma((2,)), dma((3,)), dma((2,)), dma((2, 4)), dma((2,)), dma((6,)),
+            dma((3,)), dma((3,)), dma((4,)), dma((4,)), dma((levels,)), dma((levels - 1,)),
+            dma((2,)), dma((2,)), dma((1,)), dma((1,)),
         ],
         compiler_params=pltpu.CompilerParams(
             collective_id=0, has_side_effects=True, vmem_limit_bytes=50 * 1024 * 1024

time: 35 us -> 32.5 us (0.929)
  the two profiles are of different devices: /device:TPU:0 before, /device:TPU:1 now
where the time goes in v3:
time: 32.5 us; the launch traced here: 32.3 us
  Pallas kernels  30.4 us (94%)
  local copies, waits for them, and re-layouts  1.26 us (4%)
  between operations  0.64 us (2%)
    pallas_call x1, Pallas kernels, per_device(): pl.pallas_call(functools.partial(kernel, n, strips, (tiles, kept, chips_a...  30.4 us
    unnamed x2, local copies, waits for them, and re-layouts  1.26 us

profile of v3, /device:TPU:1, one launch (start us, length us, event | category | flops | bytes accessed | tf_op | source)
XLA Modules:
  0.0 32.3 jit_solution(15745959346806817042)
XLA Ops:
  0.6 30.4 %shard_map.59 = (f32[2,2,4,16,31]{4,3,2,1,0:T(8,128)S(1)}, f32[2,2,5,2,5]{4,3,2,1,0:T(2,128)S(1)}) custom-call(bf16[2,2,2,320,344]{4,3,2,1,0:T(8,128)(2,1)} %bitcast.8, s32[2,2,5,2,5]{4,3,2,1,0:T(2,128)} %bitcast.9, s32[2,2,5,2,5]{4,3,2,1,0:T(2,128)} %bitcast.10, s32[1,2]{1,0:T(1,128)} %bitcast.11), custom_call_target="tpu_custom_call" | custom-call | tf_op jit(solution)/shard_map/pallas_call | solution.py:728
  31.0 0.6 %copy.8 = f32[2,2,2,5,5]{4,2,3,1,0:T(2,128)} copy(f32[2,2,2,5,5]{4,2,3,1,0:T(2,128)S(1)} %bitcast.7) | data formatting | bytes 1600
  31.7 0.7 %copy.9 = f32[2,31,2,4,16]{1,4,3,2,0:T(8,128)} copy(f32[2,31,2,4,16]{1,4,3,2,0:T(8,128)S(1)} %bitcast.6) | data formatting | bytes 63488

commit v4 on v3

--- a/solution.py
+++ b/solution.py
@@ -22,7 +22,7 @@
 CORES = 2
 SIDES = 2
 EARLY = 2
-SHARE = 36
+SHARE = 28
 
 epsilon = 1e-06
 COS_TERMS = (1.0, -1 / 2, 1 / 24, -1 / 720, 1 / 40320, -1 / 3628800, 1 / 479001600, -1 / 87178291200)
@@ -71,7 +71,7 @@
     coh_ref, corr_ref,
     frame, shifts_ref, fractions_ref, dates_ref, spots, line_base, col_base,
     cand, core_in, y_out, y_in, z_out, z_in, across_out, across_in, over, over_in, whole,
-    series, sent, got, cross_sums, powers, selectors, out_buf, coh_in, ordered, totals,
+    series, sent, got, cross_sums, powers, selectors, out_buf, coh_in, ordered, totals, gather,
     load_sem, small_sem, edge_send, edge_recv, core_send, core_recv, y_send, y_recv,
     z_send, z_recv, side_recv, back_recv, next_send, next_recv, coh_send, coh_recv,
 ):
@@ -106,6 +106,7 @@
         )
 
     inner = pl.ds(HALO, cols)
+    group_rows = totals.shape[2] // (tiles * GROUP)
     dates_copy = pltpu.make_async_copy(dates_hbm, dates_ref, small_sem.at[0])
     dates_copy.start()
     loads = []
@@ -448,7 +449,7 @@
             out = out.astype(f32)
             series[t, d + t, a, pl.ds(row0, CHIP_SIZE), :] = out
             power = jnp.sum((out * out).reshape(GROUP, GROUP, LANES), axis=0)
-            totals[1 + 2 * kept + d, r, pl.ds((a * tiles + t) * GROUP, GROUP), :] = power
+            totals[1 + 2 * kept + d, r, pl.ds((t * group_rows + a) * GROUP, GROUP), :] = power
 
     def resample(i, first, last):
         d, t = order[i]
@@ -495,8 +496,10 @@
     resample(2, 0, inside_cols)
     edge_wait(2)
     resample(2, inside_cols, chips_rg)
+    ref_level()
+    resample(3, 0, inside_cols)
     edge_wait(3)
-    resample(3, 0, chips_rg)
+    resample(3, inside_cols, chips_rg)
 
     looks_rg = cols // LOOK_RG
     look_rows = rows // LOOK_AZ
@@ -549,6 +552,10 @@
         return carry
 
     lax.fori_loop(0, chips_az, build_selectors, 0)
+    source = lax.broadcasted_iota(jnp.int32, gather.shape, 0)
+    target = lax.broadcasted_iota(jnp.int32, gather.shape, 1)
+    gap = source - target * LANES
+    gather[...] = jnp.where((gap >= 0) & (gap < LANES), 1.0, 0.0).astype(bf16)
 
     def correlate(t, first, count):
         for j in range(count):
@@ -556,7 +563,7 @@
             a = chip % chips_az
             r = chip // chips_az
             row = pl.multiple_of(r * CHIP_SIZE, CHIP_SIZE)
-            to = pl.ds(pl.multiple_of((a * tiles + t) * GROUP, GROUP), GROUP)
+            to = pl.ds(pl.multiple_of((t * group_rows + a) * GROUP, GROUP), GROUP)
             sums = [None] * (1 + 2 * kept)
             for g in range(chip_units):
                 ref = whole[t, chip * chip_units + g].astype(f32)
@@ -571,12 +578,14 @@
             for k, value in enumerate(sums):
                 totals[k, r, to, :] = value
 
-    ref_level()
-    tail_level()
     look(core, core, (core, 1 + core))
     inward.wait_recv()
     unpack(1, core, 2 * (1 - core))
     look(core, 1 - core, (2 * (1 - core),))
+
+    for k in range(2):
+        ref_back(k)
+    tail_level()
 
     @pl.when(has_peer)
     def _():
@@ -606,7 +615,7 @@
         )
         copy.start()
 
-    for k in range(len(steps)):
+    for k in range(2, len(steps)):
         ref_back(k)
     tail_back()
     tail_chips = chips - tail_first
@@ -617,40 +626,34 @@
     core_ag[2].wait_recv()
     correlate(1 - core, tail_first, tail_chips)
     ref_other()
+    kinds = totals.shape[0]
+
+    def finish(t):
+        sign = jnp.where(wide(group_rows) < CHIP_SIZE, 1.0, -1.0).astype(f32)
+        folded = []
+        for k in range(kinds):
+            line = []
+            for r in range(chips_rg):
+                total = None
+                for s in range(GROUP):
+                    at = pl.ds(t * (group_rows * GROUP) + s, group_rows, stride=GROUP)
+                    value = totals[k, r, at, :]
+                    total = value if total is None else total + value
+                if 1 <= k <= 2 * kept and k % 2 == 0:
+                    total = total * sign
+                line.append(total)
+            folded.append(jnp.concatenate(line, axis=1))
+        sums = split_dot(jnp.concatenate(folded, axis=0), gather[...])
+        sums = [sums[k * group_rows : (k + 1) * group_rows] for k in range(kinds)]
+        for d in range(kept):
+            scale = jnp.sqrt((sums[0] + epsilon) * (sums[1 + 2 * kept + d] + epsilon))
+            for c in range(2):
+                value = sums[1 + 2 * d + c] / scale
+                for a in range(chips_az):
+                    corr_ref[c, d, a, pl.ds(t, 1), :] = value[a : a + 1, :chips_rg]
+
     correlate(core, (1 - side) * half_chips, half_chips)
-    core_ag[1].wait_recv()
-    correlate(1 - core, (1 - side) * half_chips, half_chips)
-
-    kinds = totals.shape[0]
-    group_rows = totals.shape[2] // GROUP
-    lane16 = wide(group_rows)
-    sign = jnp.where(lane16 < CHIP_SIZE, 1.0, -1.0).astype(f32)
-    folded = []
-    for k in range(kinds):
-        line = []
-        for r in range(chips_rg):
-            total = None
-            for s in range(GROUP):
-                value = totals[k, r, pl.ds(s, group_rows, stride=GROUP), :]
-                total = value if total is None else total + value
-            if 1 <= k <= 2 * kept and k % 2 == 0:
-                total = total * sign
-            line.append(total)
-        folded.append(jnp.concatenate(line, axis=1))
-    folded = jnp.concatenate(folded, axis=0)
-    depth = chips_rg * LANES
-    source = lax.broadcasted_iota(jnp.int32, (depth, LANES), 0)
-    target = lax.broadcasted_iota(jnp.int32, (depth, LANES), 1)
-    gap = source - target * LANES
-    gather = jnp.where((gap >= 0) & (gap < LANES), 1.0, 0.0).astype(bf16)
-    sums = split_dot(folded, gather)
-    sums = [sums[k * group_rows : (k + 1) * group_rows] for k in range(kinds)]
-    for d in range(kept):
-        scale = jnp.sqrt((sums[0] + epsilon) * (sums[1 + 2 * kept + d] + epsilon))
-        for c in range(2):
-            value = sums[1 + 2 * d + c] / scale
-            for a in range(chips_az):
-                corr_ref[c, d, a] = value[a * tiles : (a + 1) * tiles, :chips_rg]
+    finish(core)
 
     others = pl.ds(0, n - 1)
     relays = remote(
@@ -672,6 +675,10 @@
                 row = c * kept * tiles * looks_rg + t * looks_rg
                 coh_ref[c, t, y] = value[row : row + looks_rg, : pairs - 1]
 
+    core_ag[1].wait_recv()
+    correlate(1 - core, (1 - side) * half_chips, half_chips)
+    finish(1 - core)
+
     relays.wait_send()
     inward.wait_send()
     for ref, sem in (
@@ -717,7 +724,7 @@
     look_rows = rows // LOOK_AZ
     share = look_rows // n
     spot_rows = -(-(kept * chips_az * tiles) // GROUP) * GROUP
-    group_rows = -(-(chips_az * tiles) // GROUP) * GROUP
+    group_rows = -(-chips_az // GROUP) * GROUP
     kinds = 1 + 3 * kept
     f32 = jnp.float32
     bf16 = jnp.bfloat16
@@ -761,7 +768,8 @@
             pltpu.VMEM((n, share, LANES), f32),
             pltpu.VMEM((n, share, LANES), f32),
             pltpu.VMEM((share, n * kept + GROUP, LANES), f32),
-            pltpu.VMEM((kinds, chips_rg, group_rows * GROUP, LANES), f32),
+            pltpu.VMEM((kinds, chips_rg, tiles * group_rows * GROUP, LANES), f32),
+            pltpu.VMEM((chips_rg * LANES, LANES), bf16),
             dma((2,)), dma((3,)), dma((2,)), dma((2, 4)), dma((2,)), dma((6,)),
             dma((3,)), dma((3,)), dma((4,)), dma((4,)), dma((levels,)), dma((levels - 1,)),
             dma((2,)), dma((2,)), dma((1,)), dma((1,)),

time: 32.5 us -> 31.2 us (0.960)
  the two profiles are of different devices: /device:TPU:1 before, /device:TPU:0 now
where the time goes in v4:
time: 31.2 us; the launch traced here: 30.9 us
  Pallas kernels  28.9 us (93%)
  local copies, waits for them, and re-layouts  1.26 us (4%)
  between operations  0.64 us (2%)
    pallas_call x1, Pallas kernels, per_device(): pl.pallas_call(functools.partial(kernel, n, strips, (tiles, kept, chips_a...  28.9 us
    unnamed x2, local copies, waits for them, and re-layouts  1.26 us

profile of v4, /device:TPU:0, one launch (start us, length us, event | category | flops | bytes accessed | tf_op | source)
XLA Modules:
  0.0 30.9 jit_solution(12806051072716719370)
XLA Ops:
  0.6 28.9 %shard_map.59 = (f32[2,2,4,16,31]{4,3,2,1,0:T(8,128)S(1)}, f32[2,2,5,2,5]{4,3,2,1,0:T(2,128)S(1)}) custom-call(bf16[2,2,2,320,344]{4,3,2,1,0:T(8,128)(2,1)} %bitcast.8, s32[2,2,5,2,5]{4,3,2,1,0:T(2,128)} %bitcast.9, s32[2,2,5,2,5]{4,3,2,1,0:T(2,128)} %bitcast.10, s32[1,2]{1,0:T(1,128)} %bitcast.11), custom_call_target="tpu_custom_call" | custom-call | tf_op jit(solution)/shard_map/pallas_call | solution.py:735
  29.6 0.6 %copy.8 = f32[2,2,2,5,5]{4,2,3,1,0:T(2,128)} copy(f32[2,2,2,5,5]{4,2,3,1,0:T(2,128)S(1)} %bitcast.7) | data formatting | bytes 1600
  30.2 0.7 %copy.9 = f32[2,31,2,4,16]{1,4,3,2,0:T(8,128)} copy(f32[2,31,2,4,16]{1,4,3,2,0:T(8,128)S(1)} %bitcast.6) | data formatting | bytes 63488

commit v5 on v4

--- a/solution.py
+++ b/solution.py
@@ -110,19 +110,21 @@
     dates_copy = pltpu.make_async_copy(dates_hbm, dates_ref, small_sem.at[0])
     dates_copy.start()
     loads = []
-    for i, t in enumerate((1 - core, core)):
+    cut = (chips_rg // 2) * CHIP_SIZE
+    parts = ((1 - core, 0, cut), (1 - core, cut, cols - cut), (core, 0, cols))
+    for i, (t, first, count) in enumerate(parts):
+        source, target = pl.ds(first, count), pl.ds(HALO + first, count)
         loads.append(
             pltpu.make_async_copy(
-                frame_hbm.at[:, t], frame.at[:, t, :, inner, :], load_sem.at[i]
+                frame_hbm.at[:, t, :, source, :], frame.at[:, t, :, target, :], load_sem.at[i]
             )
         )
-        loads[i].start()
+    loads[0].start()
+    loads[1].start()
     smalls = [
         pltpu.make_async_copy(shifts_hbm, shifts_ref, small_sem.at[1]),
         pltpu.make_async_copy(fractions_hbm, fractions_ref, small_sem.at[2]),
     ]
-    for copy in smalls:
-        copy.start()
 
     barrier = pltpu.get_barrier_semaphore()
     peer = me + 2 * core - 1
@@ -181,20 +183,22 @@
     even = [move(LANES, MARGIN, c) for c in range(2)]
     odd = [move(BAND, MARGIN + CHIP_SIZE, c) for c in range(2)]
 
-    def pick(t):
+    def pick(t, first, last):
+        count = (last - first) * CHIP_SIZE
+        here = pl.ds(HALO + first * CHIP_SIZE, count)
         dates_row = dates_ref[0:1, :]
         date_lane = lax.broadcasted_iota(jnp.int32, (1, tiles), 1)
         date = jnp.sum(jnp.where(date_lane == t, dates_row, 0), axis=1, keepdims=True)
         gains = [
-            jnp.broadcast_to(jnp.where(date == me * kept + d, 1.0, 0.0), (cols, frame.shape[4]))
+            jnp.broadcast_to(jnp.where(date == me * kept + d, 1.0, 0.0), (count, frame.shape[4]))
             .astype(bf16)
             for d in range(kept)
         ]
         parts = []
         for c in range(2):
-            total = frame[0, t, c, inner, :] * gains[0]
+            total = frame[0, t, c, here, :] * gains[0]
             for d in range(1, kept):
-                total = total + frame[d, t, c, inner, :] * gains[d]
+                total = total + frame[d, t, c, here, :] * gains[d]
             parts.append(total)
         for a in range(chips_az):
             start = (a // 2) * LANES
@@ -207,15 +211,20 @@
                 )
                 for c in range(2)
             ).astype(bf16)
-            for r in range(chips_rg):
+            for r in range(first, last):
                 unit = (r * chips_az + a) * chip_units
                 cand[t, unit : unit + chip_units] = mixed[
-                    r * CHIP_SIZE : (r + 1) * CHIP_SIZE
+                    (r - first) * CHIP_SIZE : (r - first + 1) * CHIP_SIZE
                 ].reshape(chip_units, PACK, LANES)
 
     dates_copy.wait()
     loads[0].wait()
-    pick(1 - core)
+    loads[2].start()
+    for copy in smalls:
+        copy.start()
+    pick(1 - core, 0, chips_rg // 2)
+    loads[1].wait()
+    pick(1 - core, chips_rg // 2, chips_rg)
 
     beside = jnp.minimum(strip, 1) + jnp.minimum(strips - 1 - strip, 1)
     linked = jnp.where(has_peer, 1, 0)
@@ -259,8 +268,8 @@
         def _():
             edges[i][1].wait_recv()
 
-    loads[1].wait()
-    pick(core)
+    loads[2].wait()
+    pick(core, 0, chips_rg)
 
     def level_piece(y, z):
         return pl.ds(y * half_units + z * piece, piece)
@@ -470,7 +479,7 @@
         @pl.when(has_peer)
         def _():
             for r in range(first, last):
-                outward[r].start()
+                outward[(r + 1) % chips_rg].start()
 
     def outward_all():
         return remote(sent.at[0], got.at[0], next_send.at[0], next_recv.at[0], {"date": peer})
@@ -484,15 +493,16 @@
     edge_wait(0)
     resample(0, inside_cols, chips_rg)
     ref_side(1)
+    outward_start(0, EARLY)
     resample(1, 0, inside_cols)
     for k in range(2, len(steps)):
         ref_side(k)
-    outward_start(0, EARLY)
+    outward_start(EARLY, 3)
     edge_wait(1)
     resample(1, inside_cols, chips_rg)
     inward.start()
     tail_side()
-    outward_start(EARLY, chips_rg)
+    outward_start(3, chips_rg)
     resample(2, 0, inside_cols)
     edge_wait(2)
     resample(2, inside_cols, chips_rg)
@@ -770,7 +780,7 @@
             pltpu.VMEM((share, n * kept + GROUP, LANES), f32),
             pltpu.VMEM((kinds, chips_rg, tiles * group_rows * GROUP, LANES), f32),
             pltpu.VMEM((chips_rg * LANES, LANES), bf16),
-            dma((2,)), dma((3,)), dma((2,)), dma((2, 4)), dma((2,)), dma((6,)),
+            dma((3,)), dma((3,)), dma((2,)), dma((2, 4)), dma((2,)), dma((6,)),
             dma((3,)), dma((3,)), dma((4,)), dma((4,)), dma((levels,)), dma((levels - 1,)),
             dma((2,)), dma((2,)), dma((1,)), dma((1,)),
         ],

time: 31.2 us -> 30.5 us (0.978)
  Pallas kernels: 28.9 us -> 28.4 us
    pallas_call x1, Pallas kernels: 28.9 us -> 28.4 us  [per_device(): pl.pallas_call(functools.partial(kernel, n, strips, (tiles, kept, chips_a...]
where the time goes in v5:
time: 30.5 us; the launch traced here: 30.3 us
  Pallas kernels  28.4 us (93%)
  local copies, waits for them, and re-layouts  1.26 us (4%)
  between operations  0.64 us (2%)
    pallas_call x1, Pallas kernels, per_device(): pl.pallas_call(functools.partial(kernel, n, strips, (tiles, kept, chips_a...  28.4 us
    unnamed x2, local copies, waits for them, and re-layouts  1.26 us

profile of v5, /device:TPU:0, one launch (start us, length us, event | category | flops | bytes accessed | tf_op | source)
XLA Modules:
  0.0 30.3 jit_solution(6385715072515059634)
XLA Ops:
  0.6 28.4 %shard_map.59 = (f32[2,2,4,16,31]{4,3,2,1,0:T(8,128)S(1)}, f32[2,2,5,2,5]{4,3,2,1,0:T(2,128)S(1)}) custom-call(bf16[2,2,2,320,344]{4,3,2,1,0:T(8,128)(2,1)} %bitcast.8, s32[2,2,5,2,5]{4,3,2,1,0:T(2,128)} %bitcast.9, s32[2,2,5,2,5]{4,3,2,1,0:T(2,128)} %bitcast.10, s32[1,2]{1,0:T(1,128)} %bitcast.11), custom_call_target="tpu_custom_call" | custom-call | tf_op jit(solution)/shard_map/pallas_call | solution.py:745
  29.1 0.6 %copy.8 = f32[2,2,2,5,5]{4,2,3,1,0:T(2,128)} copy(f32[2,2,2,5,5]{4,2,3,1,0:T(2,128)S(1)} %bitcast.7) | data formatting | bytes 1600
  29.7 0.7 %copy.9 = f32[2,31,2,4,16]{1,4,3,2,0:T(8,128)} copy(f32[2,31,2,4,16]{1,4,3,2,0:T(8,128)S(1)} %bitcast.6) | data formatting | bytes 63488

commit v6 on v5

--- a/solution.py
+++ b/solution.py
@@ -504,9 +504,9 @@
     tail_side()
     outward_start(3, chips_rg)
     resample(2, 0, inside_cols)
+    ref_level()
     edge_wait(2)
     resample(2, inside_cols, chips_rg)
-    ref_level()
     resample(3, 0, inside_cols)
     edge_wait(3)
     resample(3, inside_cols, chips_rg)

time: 30.5 us -> 30.5 us (level)
  no operation moved by 1% of the time
where the time goes in v6:
time: 30.5 us; the launch traced here: 30.3 us
  Pallas kernels  28.4 us (93%)
  local copies, waits for them, and re-layouts  1.26 us (4%)
  between operations  0.64 us (2%)
    pallas_call x1, Pallas kernels, per_device(): pl.pallas_call(functools.partial(kernel, n, strips, (tiles, kept, chips_a...  28.4 us
    unnamed x2, local copies, waits for them, and re-layouts  1.26 us

profile of v6, /device:TPU:0, one launch (start us, length us, event | category | flops | bytes accessed | tf_op | source)
XLA Modules:
  0.0 30.3 jit_solution(11385480877398779613)
XLA Ops:
  0.6 28.4 %shard_map.59 = (f32[2,2,4,16,31]{4,3,2,1,0:T(8,128)S(1)}, f32[2,2,5,2,5]{4,3,2,1,0:T(2,128)S(1)}) custom-call(bf16[2,2,2,320,344]{4,3,2,1,0:T(8,128)(2,1)} %bitcast.8, s32[2,2,5,2,5]{4,3,2,1,0:T(2,128)} %bitcast.9, s32[2,2,5,2,5]{4,3,2,1,0:T(2,128)} %bitcast.10, s32[1,2]{1,0:T(1,128)} %bitcast.11), custom_call_target="tpu_custom_call" | custom-call | tf_op jit(solution)/shard_map/pallas_call | solution.py:745
  29.1 0.6 %copy.8 = f32[2,2,2,5,5]{4,2,3,1,0:T(2,128)} copy(f32[2,2,2,5,5]{4,2,3,1,0:T(2,128)S(1)} %bitcast.7) | data formatting | bytes 1600
  29.7 0.7 %copy.9 = f32[2,31,2,4,16]{1,4,3,2,0:T(8,128)} copy(f32[2,31,2,4,16]{1,4,3,2,0:T(8,128)S(1)} %bitcast.6) | data formatting | bytes 63488
